TPU v7x, 512 devices: a whole 4x8x8 slice. The times are simulated.
512 devices in a mesh: grp: 4 (over y_lo, core), src: 16 (over y_hi, x), rcv: 8 (over z).
Axes of the slice: x: 4, y: 8 (y_hi: 4, y_lo: 2; y = y_hi * 2 + y_lo), z: 8, core: 2. Of those that a mesh axis runs over, the one named last changes fastest.
Arguments:
- recorded: bfloat16 [4, 2, 4096, 4096], P('grp', None, 'src', 'rcv'), parts along dimension 0, as said below
- aperture: int32 [128, 32, 3], P(('grp', 'src'), 'rcv'), parts along dimension 0, may hold values from 0 to 32, as said below
Outputs:
- multiples: float32 [4, 2, 4096, 4096], P('grp', None, 'src', 'rcv'), parts along dimension 0
There are 4 independent parts, one for each index of `grp`. A program takes and returns all parts, laid end to end along the dimension named above; each array names one. Nothing has to cross between parts.
Inputs may be any that keep to these rules, and one draw needn't show every extreme that they name: The data obey reciprocity: recorded(f, c, q, j) equals recorded(f, c, j, q). `aperture`: field 1 is from 4 to 32, field 0 plus field 1 is at most 32, field 2 is from 0 to 2. In every draw some tile pair spans all 32 k-blocks and some has taper width 2.
All inputs are finite; a program needn't handle non-finite values.
Results may differ from a plain program's by a relative error of at most 0.0004.
Values may be sent and summed in bfloat16 or wider, within the bound.
No kernel may reach another device: no remote copies, remote signals or barrier semaphores. Data moves between devices by JAX's collectives and lax.ppermute only.
A program may use at most 64 MiB of HBM per device.

v0:
```python
import jax
import jax.numpy as jnp
from jax import lax
from jax.sharding import PartitionSpec as P

NB = 32
TILE = 128


def tile_weights(aperture):
    block_ids = jnp.arange(NB, dtype=jnp.int32)
    offset = block_ids[None, None, :] - aperture[..., 0:1]
    extent = aperture[..., 1:2]
    taper_width = aperture[..., 2:3]
    margin = jnp.minimum(offset, extent - 1 - offset)
    ramped = jnp.minimum(
        1.0, (margin + 1).astype(jnp.float32) / (taper_width + 1).astype(jnp.float32)
    )
    return jnp.where((offset >= 0) & (offset < extent), ramped, 0.0)


def shards(recorded, aperture):
    slices = recorded.shape[0]
    own_rows = recorded.shape[2]
    own_cols = recorded.shape[3]
    row_tiles = own_rows // TILE
    col_tiles = own_cols // TILE
    weights = tile_weights(aperture)
    block_ids = jnp.arange(NB, dtype=jnp.int32)
    left_panel = lax.all_gather(recorded, "rcv", axis=3, tiled=True)

    def block_terms(incoming, first_row, span_rows, tile_weight):
        part_left = lax.dynamic_slice_in_dim(left_panel, first_row, span_rows, 3)
        part_left = part_left.reshape(slices, 2, row_tiles, TILE, span_rows)
        block_of = (first_row + jnp.arange(span_rows, dtype=jnp.int32)) // TILE
        row_weights = jnp.sum(
            jnp.where(block_of[:, None] == block_ids[None, :], tile_weight[:, :, None, :], 0.0),
            axis=-1,
        )
        scaled = (part_left[:, :, :, None, :, :] * row_weights[None, None, :, :, None, :]).astype(
            jnp.bfloat16
        )
        sub_tiles = tile_weight.shape[1]
        right_tiles = incoming.reshape(slices, 2, span_rows, sub_tiles, TILE)
        products = jnp.einsum(
            "fastik,fbktj->fabstij", scaled, right_tiles, preferred_element_type=jnp.float32
        )
        return jnp.stack(
            [products[:, 0, 0] - products[:, 1, 1], products[:, 0, 1] + products[:, 1, 0]], 1
        )

    empty = jnp.zeros((slices, 2, row_tiles, col_tiles, TILE, TILE), jnp.float32)
    incoming = lax.all_gather(recorded, "src", axis=2, tiled=True)
    extent = incoming.shape[2]

    def add_block(first_row, span_rows, running):
        portion = lax.dynamic_slice_in_dim(incoming, first_row, span_rows, 2)
        return running + block_terms(portion, first_row, span_rows, weights)

    sweeps = extent // TILE
    summed = lax.fori_loop(
        0, sweeps, lambda number, running: add_block(number * TILE, TILE, running), empty
    )
    return summed.transpose(0, 1, 2, 4, 3, 5).reshape(slices, 2, own_rows, own_cols)


def solution(mesh):
    in_specs = (P("grp", None, "src", "rcv"), P(("grp", "src"), "rcv", None))
    out_specs = P("grp", None, "src", "rcv")
    return jax.shard_map(shards, mesh=mesh, in_specs=in_specs, out_specs=out_specs, check_vma=False)
```

profile of v0, /device:TPU:1, one launch (start us, length us, event | category | flops | bytes accessed | tf_op | source)
XLA Modules:
  0.0 312.6 jit_solution(3568070417147690657)
XLA Ops:
  7.3 2.0 copy.15
  10.1 63.1 %all-gather.5.cloned.1.call-done = bf16[1,2,256,4096]{3,2,1,0:T(8,128)(2,1)} async-done(((bf16[1,2,256,512]{3,2,1,0:T(8,128)(2,1)}), bf16[1,2,256,4096]{3,2,1,0:T(8,128)(2,1)}) %all-gather.5.cloned.1.call-update) | async-done | bytes 4194320 | tf_op jit(solution)/shard_map/all_gather | solution.py:30
  73.2 131.2 %all-gather.3.cloned.1.call-done = bf16[1,2,4096,512]{2,3,1,0:T(8,128)(2,1)} async-done(((bf16[1,2,256,512]{2,3,1,0:T(8,128)(2,1)}), bf16[1,2,4096,512]{2,3,1,0:T(8,128)(2,1)}) %all-gather.3.cloned.1.call-update) | async-done | bytes 8388624 | tf_op jit(solution)/shard_map/all_gather | solution.py:53
  204.4 99.5 %while.16 = (s32[]{:T(128)}, f32[1,2,2,4,128,128]{4,5,2,3,1,0:T(8,128)S(1)}, bf16[1,2,4096,512]{2,3,1,0:T(8,128)(2,1)}, bf16[1,2,256,4096]{3,2,1,0:T(8,128)(2,1)...) while((s32[]{:T(128)}, ...), condition=%wide.region_2.3_spmd.clone, body=%wide.region_0.2_spmd.clone.sunk | while | flops 135929600 | bytes 10120505 | solution.py:61
  205.4 1.0 constant_dynamic-slice_fusion.5
  208.5 1.0 constant_dynamic-slice_fusion.5
  211.6 1.0 constant_dynamic-slice_fusion.5
  214.7 1.0 constant_dynamic-slice_fusion.5
  217.8 1.0 constant_dynamic-slice_fusion.5
  220.9 1.0 constant_dynamic-slice_fusion.5
  224.0 1.0 constant_dynamic-slice_fusion.5
  227.1 1.0 constant_dynamic-slice_fusion.5
  230.2 1.0 constant_dynamic-slice_fusion.5
  233.4 1.0 constant_dynamic-slice_fusion.5
  236.5 1.0 constant_dynamic-slice_fusion.5
  239.6 1.0 constant_dynamic-slice_fusion.5
  242.7 1.0 constant_dynamic-slice_fusion.5
  245.8 1.0 constant_dynamic-slice_fusion.5
  248.9 1.0 constant_dynamic-slice_fusion.5
  252.0 1.0 constant_dynamic-slice_fusion.5
  255.1 1.0 constant_dynamic-slice_fusion.5
  258.3 1.0 constant_dynamic-slice_fusion.5
  267.6 1.0 constant_dynamic-slice_fusion.5
  273.8 1.0 constant_dynamic-slice_fusion.5
  276.9 1.0 constant_dynamic-slice_fusion.5
  280.0 1.0 constant_dynamic-slice_fusion.5
  283.1 1.0 constant_dynamic-slice_fusion.5
  286.3 1.0 constant_dynamic-slice_fusion.5
  289.4 1.0 constant_dynamic-slice_fusion.5
  295.6 1.0 constant_dynamic-slice_fusion.5
  301.8 1.0 constant_dynamic-slice_fusion.5
  304.4 1.4 reshape.136
  (364 shorter events, 72.1 us)
Async XLA Ops:
  6.5 66.7 %all-gather.5.cloned.1.call-start = ((), (), s32[]{:S(2)}) async-start(), calls=%async_computation.1 | async-start | bytes 4718592 | tf_op jit(solution)/shard_map/all_gather | solution.py:30
  7.3 197.1 %all-gather.3.cloned.1.call-start = ((), (), s32[]{:S(2)}) async-start(), calls=%async_computation | async-start | bytes 8912896 | tf_op jit(solution)/shard_map/all_gather | solution.py:53
Sparse Core Ops, SparseCore 0:
  9.4 63.7 all-gather.4
  76.2 128.1 all-gather.2
where the time goes:
time: 314 us; the launch traced here: 313 us
  waiting for transfers between devices  195 us (62%)
  local copies, waits for them, and re-layouts  64.6 us (21%)
  other arithmetic  22.6 us (7%)
  matrix products  13.9 us (4%)
  between operations  13.4 us (4%)
    all_gather x1, waiting for transfers between devices, shards(): incoming = lax.all_gather(recorded, 'src', axis=2, tiled=True)  131 us
    all_gather x1, waiting for transfers between devices, shards(): left_panel = lax.all_gather(recorded, 'rcv', axis=3, tiled=True)  63.1 us
    dynamic_slice x32, local copies, waits for them, and re-layouts, add_block(): portion = lax.dynamic_slice_in_dim(incoming, first_row, span_rows, 2)  31.2 us
    dynamic_slice x32, local copies, waits for them, and re-layouts, block_terms(): part_left = lax.dynamic_slice_in_dim(left_panel, first_row, span_rows, 3)  29.4 us
    dot_general x32, matrix products, block_terms(): jnp.einsum('fastik,fbktj->fabstij', scaled, right_tiles, preferred_elemen...  13.9 us
    add x32, other arithmetic, add_block(): return running + block_terms(portion, first_row, span_rows, weights)  10.7 us
  transfers between devices with their start and end apart: 2, of which 2 were waited for; matrix products, arithmetic and copies ran while one was open for 1% of the time, Pallas kernels for 0%

commit v1 on v0

v1 whole, which is shorter than its diff:
```python
import functools

import jax
import jax.numpy as jnp
from jax import lax
from jax.experimental import pallas as pl
from jax.experimental.pallas import tpu as pltpu
from jax.sharding import PartitionSpec as P

NB = 32
TILE = 128
GRID_Y = 4
GRID_X = 4
ROWS = 256
COLS = 512


def tile_weights(aperture):
    block_ids = jnp.arange(NB, dtype=jnp.int32)
    offset = block_ids[None, None, :] - aperture[..., 0:1]
    extent = aperture[..., 1:2]
    taper_width = aperture[..., 2:3]
    margin = jnp.minimum(offset, extent - 1 - offset)
    ramped = jnp.minimum(
        1.0, (margin + 1).astype(jnp.float32) / (taper_width + 1).astype(jnp.float32)
    )
    return jnp.where((offset >= 0) & (offset < extent), ramped, 0.0)


def shift(block, dy, dx):
    pairs = [
        (GRID_X * y + x, GRID_X * ((y + dy) % GRID_Y) + (x + dx) % GRID_X)
        for y in range(GRID_Y)
        for x in range(GRID_X)
    ]
    return lax.ppermute(block, "src", pairs)


def accumulate(has_base, pieces, weights, places, left, *refs):
    if has_base:
        base, refs = refs[0], refs[1:]
    blocks, out = refs[:pieces], refs[pieces]
    for tile in range(COLS // TILE):
        cols = slice(tile * TILE, (tile + 1) * TILE)
        total = None
        for number in range(pieces):
            place = places[number]
            start = pl.multiple_of(place * ROWS, ROWS)
            parts = []
            for half in range(ROWS // TILE):
                lanes = pl.ds(pl.multiple_of(start + half * TILE, TILE), TILE)
                rows = []
                for part in range(2):
                    for a in range(2):
                        value = left[0, part, a * TILE : (a + 1) * TILE, lanes]
                        weight = weights[a * 4 + tile, 2 * place + half]
                        rows.append((value.astype(jnp.float32) * weight).astype(jnp.bfloat16))
                parts.append(jnp.concatenate(rows, axis=0))
            scaled = jnp.concatenate(parts, axis=1)
            block = blocks[number]
            right = jnp.concatenate([block[0, 0, :, cols], block[0, 1, :, cols]], axis=1)
            product = jnp.dot(scaled, right, preferred_element_type=jnp.float32)
            total = product if total is None else total + product
        real = total[:ROWS, :TILE] - total[ROWS:, TILE:]
        imag = total[:ROWS, TILE:] + total[ROWS:, :TILE]
        if has_base:
            real = real + base[0, 0, :, cols]
            imag = imag + base[0, 1, :, cols]
        out[0, 0, :, cols] = real
        out[0, 1, :, cols] = imag


def add_blocks(weights, places, left, blocks, base=None):
    count = len(blocks)
    smem = pl.BlockSpec(memory_space=pltpu.SMEM)
    vmem = pl.BlockSpec(memory_space=pltpu.VMEM)
    extra = () if base is None else (base,)
    return pl.pallas_call(
        functools.partial(accumulate, base is not None, count),
        out_shape=jax.ShapeDtypeStruct((1, 2, ROWS, COLS), jnp.float32),
        in_specs=[smem, smem] + [vmem] * (1 + len(extra) + count),
        out_specs=vmem,
        compiler_params=pltpu.CompilerParams(vmem_limit_bytes=40 << 20),
        cost_estimate=pl.CostEstimate(
            flops=count * 2 * 4 * ROWS * ROWS * COLS,
            bytes_accessed=count * (1 << 19) + (5 << 20),
            transcendentals=0,
        ),
    )(weights, places, left, *extra, *blocks)


def shards(recorded, aperture):
    weights = tile_weights(aperture).reshape(8, NB)
    own = recorded
    left = lax.all_gather(recorded, "rcv", axis=3, tiled=True)
    got = {(0, 0): own}
    got[1, 0] = shift(own, 1, 0)
    got[3, 0] = shift(own, -1, 0)
    got[0, 1] = shift(own, 0, 1)
    got[0, 3] = shift(own, 0, -1)
    far = [shift(got[0, 1][:, :1], 0, 1), shift(got[0, 3][:, 1:], 0, -1)]
    got[0, 2] = jnp.concatenate(far, axis=1)
    far = [shift(got[1, 0][:, :1], 1, 0), shift(got[3, 0][:, 1:], -1, 0)]
    got[2, 0] = jnp.concatenate(far, axis=1)
    for row in (1, 3):
        got[row, 1] = shift(got[row, 0], 0, 1)
        got[row, 3] = shift(got[row, 0], 0, -1)
    got[1, 2] = shift(got[0, 2], 1, 0)
    got[3, 2] = shift(got[0, 2], -1, 0)
    got[2, 1] = shift(got[2, 0], 0, 1)
    got[2, 3] = shift(got[2, 0], 0, -1)
    far = [shift(got[2, 1][:, :1], 0, 1), shift(got[2, 3][:, 1:], 0, -1)]
    got[2, 2] = jnp.concatenate(far, axis=1)

    source = lax.axis_index("src")
    y, x = source // GRID_X, source % GRID_X

    def places(keys):
        return jnp.stack([(y - dy) % GRID_Y * GRID_X + (x - dx) % GRID_X for dy, dx in keys])

    early = [(0, 0), (1, 0), (3, 0), (0, 1), (0, 3), (0, 2), (2, 0), (1, 1), (1, 3), (3, 1), (3, 3)]
    late = [(1, 2), (3, 2), (2, 1), (2, 3), (2, 2)]
    total = add_blocks(weights, places(early), left, [got[k] for k in early])
    return add_blocks(weights, places(late), left, [got[k] for k in late], total)


def solution(mesh):
    in_specs = (P("grp", None, "src", "rcv"), P(("grp", "src"), "rcv", None))
    out_specs = P("grp", None, "src", "rcv")
    return jax.shard_map(shards, mesh=mesh, in_specs=in_specs, out_specs=out_specs, check_vma=False)
```

time: 314 us -> 149 us (0.47)
  the two profiles are of different devices: /device:TPU:1 before, /device:TPU:456 now
where the time goes in v1:
time: 149 us; the launch traced here: 148 us
  starting transfers between devices  66.9 us (45%)
  waiting for transfers between devices  41.6 us (28%)
  local copies, waits for them, and re-layouts  15.5 us (10%)
  between operations  13.8 us (9%)
  Pallas kernels  8.7 us (6%)
    ppermute x18, starting transfers between devices, shift(): return lax.ppermute(block, 'src', pairs)  66.9 us
    ppermute x18, waiting for transfers between devices, shift(): return lax.ppermute(block, 'src', pairs)  40.9 us
    unnamed x34, local copies, waits for them, and re-layouts  10.4 us
    pallas_call x2, Pallas kernels, add_blocks(): pl.pallas_call(functools.partial(accumulate, base is not None, count), ou...  8.7 us
  transfers between devices with their start and end apart: 19, of which 6 were waited for; matrix products, arithmetic and copies ran while one was open for 5% of the time, Pallas kernels for 3%

profile of v1, /device:TPU:456, one launch (start us, length us, event | category | flops | bytes accessed | tf_op | source)
XLA Modules:
  0.0 147.8 jit_solution(746482507038029611)
XLA Ops:
  7.3 4.5 %collective-permute-start = (bf16[1,2,256,512]{3,2,1,0:T(8,128)(2,1)}, bf16[1,2,256,512]{3,2,1,0:T(8,128)(2,1)S(1)}, u32[]{:S(2)}, u32[]{:S(2)}) collective-permute-start(bf16[1,2,256,512]{3,2,1,0:T(8,128)(2,1)} %refs_0_.1), channel_id=1, source_target_pairs={{0,32},{8,40},{16,48},{24,56},{32,64},{40,72},{48,80},{56,88},{64,... | collective-permute-start | bytes 1572872 | tf_op jit(solution)/shard_map/ppermute | solution.py:36
  11.8 3.5 %collective-permute-start.1 = (bf16[1,2,256,512]{3,2,1,0:T(8,128)(2,1)}, bf16[1,2,256,512]{3,2,1,0:T(8,128)(2,1)S(1)}, u32[]{:S(2)}, u32[]{:S(2)}) collective-permute-start(bf16[1,2,256,512]{3,2,1,0:T(8,128)(2,1)} %refs_0_.1), channel_id=1, source_target_pairs={{0,96},{8,104},{16,112},{24,120},{32,0},{40,8},{48,16},{56,24},{64... | collective-permute-start | bytes 1572872 | tf_op jit(solution)/shard_map/ppermute | solution.py:36
  15.2 21.2 %collective-permute-done.refs_1_ = bf16[1,2,256,512]{3,2,1,0:T(8,128)(2,1)S(1)} collective-permute-done((bf16[1,2,256,512]{3,2,1,0:T(8,128)(2,1)}, bf16[1,2,256,512]{3,2,1,0:T(8,128)(2,1)S(1)}, u32[]{:S(2)}, u32[]{:S(2)}) %collective-permute-start) | collective-permute-done | bytes 524320 | tf_op jit(solution)/shard_map/ppermute | solution.py:36
  36.5 3.3 %collective-permute-start.6 = (bf16[1,1,256,512]{3,2,1,0:T(8,128)(2,1)S(1)}, bf16[1,1,256,512]{3,2,1,0:T(8,128)(2,1)S(1)}, u32[]{:S(2)}, u32[]{:S(2)}) collective-permute-start(bf16[1,1,256,512]{3,2,1,0:T(8,128)(2,1)S(1)} %slice.38), channel_id=1, source_target_pairs={{0,32},{8,40},{16,48},{24,56},{32,64},{40,72},{48,80},{56,88},{64,... | collective-permute-start | bytes 786440 | tf_op jit(solution)/shard_map/ppermute | solution.py:36
  39.8 4.6 %collective-permute-start.7 = (bf16[1,1,256,512]{3,2,1,0:T(8,128)(2,1)S(1)}, bf16[1,1,256,512]{3,2,1,0:T(8,128)(2,1)S(1)}, u32[]{:S(2)}, u32[]{:S(2)}) collective-permute-start(bf16[1,1,256,512]{3,2,1,0:T(8,128)(2,1)S(1)} %slice.39), channel_id=1, source_target_pairs={{0,96},{8,104},{16,112},{24,120},{32,0},{40,8},{48,16},{56,24},{64... | collective-permute-start | bytes 786440 | tf_op jit(solution)/shard_map/ppermute | solution.py:36
  44.5 3.4 %collective-permute-start.2 = (bf16[1,2,256,512]{3,2,1,0:T(8,128)(2,1)}, bf16[1,2,256,512]{3,2,1,0:T(8,128)(2,1)S(1)}, u32[]{:S(2)}, u32[]{:S(2)}) collective-permute-start(bf16[1,2,256,512]{3,2,1,0:T(8,128)(2,1)} %refs_0_.1), channel_id=1, source_target_pairs={{0,8},{8,16},{16,24},{24,0},{32,40},{40,48},{48,56},{56,32},{64,72... | collective-permute-start | bytes 1572872 | tf_op jit(solution)/shard_map/ppermute | solution.py:36
  47.9 3.7 %collective-permute-start.3 = (bf16[1,2,256,512]{3,2,1,0:T(8,128)(2,1)}, bf16[1,2,256,512]{3,2,1,0:T(8,128)(2,1)S(1)}, u32[]{:S(2)}, u32[]{:S(2)}) collective-permute-start(bf16[1,2,256,512]{3,2,1,0:T(8,128)(2,1)} %refs_0_.1), channel_id=1, source_target_pairs={{0,24},{8,0},{16,8},{24,16},{32,56},{40,32},{48,40},{56,48},{64,88... | collective-permute-start | bytes 1572872 | tf_op jit(solution)/shard_map/ppermute | solution.py:36
  52.5 4.7 %collective-permute-start.15 = (bf16[1,2,256,512]{3,2,1,0:T(8,128)(2,1)S(1)}, bf16[1,2,256,512]{3,2,1,0:T(8,128)(2,1)S(1)}, u32[]{:S(2)}, u32[]{:S(2)}) collective-permute-start(bf16[1,2,256,512]{3,2,1,0:T(8,128)(2,1)S(1)} %constant_dynamic-update-slice_fusion.2.refs_6_), channel_id=1, source_target_pairs={{0,24},{8,0},{16,8},{24,16},{32,56},{40,32},{48,40},{56,48},{64,88... | collective-permute-start | bytes 1572872 | tf_op jit(solution)/shard_map/ppermute | solution.py:36
  57.1 1.9 %collective-permute-start.14 = (bf16[1,2,256,512]{3,2,1,0:T(8,128)(2,1)S(1)}, bf16[1,2,256,512]{3,2,1,0:T(8,128)(2,1)S(1)}, u32[]{:S(2)}, u32[]{:S(2)}) collective-permute-start(bf16[1,2,256,512]{3,2,1,0:T(8,128)(2,1)S(1)} %constant_dynamic-update-slice_fusion.2.refs_6_), channel_id=1, source_target_pairs={{0,8},{8,16},{16,24},{24,0},{32,40},{40,48},{48,56},{56,32},{64,72... | collective-permute-start | bytes 1572872 | tf_op jit(solution)/shard_map/ppermute | solution.py:36
  59.1 2.7 %collective-permute-start.8 = (bf16[1,2,256,512]{3,2,1,0:T(8,128)(2,1)S(1)}, bf16[1,2,256,512]{3,2,1,0:T(8,128)(2,1)}, u32[]{:S(2)}, u32[]{:S(2)}) collective-permute-start(bf16[1,2,256,512]{3,2,1,0:T(8,128)(2,1)S(1)} %collective-permute-done.refs_1_), channel_id=1, source_target_pairs={{0,8},{8,16},{16,24},{24,0},{32,40},{40,48},{48,56},{56,32},{64,72... | collective-permute-start | bytes 1572872 | tf_op jit(solution)/shard_map/ppermute | solution.py:36
  62.5 3.4 %collective-permute-start.4 = (bf16[1,1,256,512]{3,2,1,0:T(8,128)(2,1)}, bf16[1,1,256,512]{3,2,1,0:T(8,128)(2,1)S(1)}, u32[]{:S(2)}, u32[]{:S(2)}) collective-permute-start(bf16[1,1,256,512]{3,2,1,0:T(8,128)(2,1)} %slice.36), channel_id=1, source_target_pairs={{0,8},{8,16},{16,24},{24,0},{32,40},{40,48},{48,56},{56,32},{64,72... | collective-permute-start | bytes 786440 | tf_op jit(solution)/shard_map/ppermute | solution.py:36
  66.6 3.8 %collective-permute-start.5 = (bf16[1,1,256,512]{3,2,1,0:T(8,128)(2,1)}, bf16[1,1,256,512]{3,2,1,0:T(8,128)(2,1)}, u32[]{:S(2)}, u32[]{:S(2)}) collective-permute-start(bf16[1,1,256,512]{3,2,1,0:T(8,128)(2,1)} %slice.37), channel_id=1, source_target_pairs={{0,24},{8,0},{16,8},{24,16},{32,56},{40,32},{48,40},{56,48},{64,88... | collective-permute-start | bytes 786440 | tf_op jit(solution)/shard_map/ppermute | solution.py:36
  70.4 5.7 %collective-permute-done.15.refs_4_ = bf16[1,2,256,512]{3,2,1,0:T(8,128)(2,1)S(1)} collective-permute-done((bf16[1,2,256,512]{3,2,1,0:T(8,128)(2,1)S(1)}, bf16[1,2,256,512]{3,2,1,0:T(8,128)(2,1)S(1)}, u32[]{:S(2)}, u32[]{:S(2)}) %collective-permute-start.15) | collective-permute-done | bytes 524320 | tf_op jit(solution)/shard_map/ppermute | solution.py:36
  76.9 4.9 %collective-permute-start.17 = (bf16[1,1,256,512]{3,2,1,0:T(8,128)(2,1)}, bf16[1,1,256,512]{3,2,1,0:T(8,128)(2,1)}, u32[]{:S(2)}, u32[]{:S(2)}) collective-permute-start(bf16[1,1,256,512]{3,2,1,0:T(8,128)(2,1)} %slice.41), channel_id=1, source_target_pairs={{0,24},{8,0},{16,8},{24,16},{32,56},{40,32},{48,40},{56,48},{64,88... | collective-permute-start | bytes 786440 | tf_op jit(solution)/shard_map/ppermute | solution.py:36
  83.2 1.9 %collective-permute-start.16 = (bf16[1,1,256,512]{3,2,1,0:T(8,128)(2,1)}, bf16[1,1,256,512]{3,2,1,0:T(8,128)(2,1)}, u32[]{:S(2)}, u32[]{:S(2)}) collective-permute-start(bf16[1,1,256,512]{3,2,1,0:T(8,128)(2,1)} %slice.40), channel_id=1, source_target_pairs={{0,8},{8,16},{16,24},{24,0},{32,40},{40,48},{48,56},{56,32},{64,72... | collective-permute-start | bytes 786440 | tf_op jit(solution)/shard_map/ppermute | solution.py:36
  85.8 6.2 %collective-permute-done.4 = bf16[1,1,256,512]{3,2,1,0:T(8,128)(2,1)S(1)} collective-permute-done((bf16[1,1,256,512]{3,2,1,0:T(8,128)(2,1)}, bf16[1,1,256,512]{3,2,1,0:T(8,128)(2,1)S(1)}, u32[]{:S(2)}, u32[]{:S(2)}) %collective-permute-start.4) | collective-permute-done | bytes 262176 | tf_op jit(solution)/shard_map/ppermute | solution.py:36
  92.0 1.9 %collective-permute-start.9 = (bf16[1,2,256,512]{3,2,1,0:T(8,128)(2,1)S(1)}, bf16[1,2,256,512]{3,2,1,0:T(8,128)(2,1)S(1)}, u32[]{:S(2)}, u32[]{:S(2)}) collective-permute-start(bf16[1,2,256,512]{3,2,1,0:T(8,128)(2,1)S(1)} %collective-permute-done.refs_1_), channel_id=1, source_target_pairs={{0,24},{8,0},{16,8},{24,16},{32,56},{40,32},{48,40},{56,48},{64,88... | collective-permute-start | bytes 1572872 | tf_op jit(solution)/shard_map/ppermute | solution.py:36
  93.9 3.9 %collective-permute-start.10 = (bf16[1,2,256,512]{3,2,1,0:T(8,128)(2,1)S(1)}, bf16[1,2,256,512]{3,2,1,0:T(8,128)(2,1)S(1)}, u32[]{:S(2)}, u32[]{:S(2)}) collective-permute-start(bf16[1,2,256,512]{3,2,1,0:T(8,128)(2,1)S(1)} %collective-permute-done.1.refs_2_), channel_id=1, source_target_pairs={{0,8},{8,16},{16,24},{24,0},{32,40},{40,48},{48,56},{56,32},{64,72... | collective-permute-start | bytes 1572872 | tf_op jit(solution)/shard_map/ppermute | solution.py:36
  97.8 3.1 %collective-permute-start.11 = (bf16[1,2,256,512]{3,2,1,0:T(8,128)(2,1)S(1)}, bf16[1,2,256,512]{3,2,1,0:T(8,128)(2,1)S(1)}, u32[]{:S(2)}, u32[]{:S(2)}) collective-permute-start(bf16[1,2,256,512]{3,2,1,0:T(8,128)(2,1)S(1)} %collective-permute-done.1.refs_2_), channel_id=1, source_target_pairs={{0,24},{8,0},{16,8},{24,16},{32,56},{40,32},{48,40},{56,48},{64,88... | collective-permute-start | bytes 1572872 | tf_op jit(solution)/shard_map/ppermute | solution.py:36
  101.7 1.7 %constant_dynamic-update-slice_fusion.refs_5_ = bf16[1,2,256,512]{3,2,1,0:T(8,128)(2,1)} fusion(bf16[1,2,256,512]{3,2,1,0:T(8,128)(2,1)} %constant_dynamic-update-slice_fusion.1, bf16[1,1,256,512]{3,2,1,0:T(8,128)(2,1)} %collective-permute-done.5), kind=kLoop, calls=%fused_computation.1 | loop fusion | bytes 524288 | tf_op jit(solution)/shard_map/concatenate | solution.py:102
  103.4 9.8 %collective-permute-start.12 = (bf16[1,2,256,512]{3,2,1,0:T(8,128)(2,1)}, bf16[1,2,256,512]{3,2,1,0:T(8,128)(2,1)}, u32[]{:S(2)}, u32[]{:S(2)}) collective-permute-start(bf16[1,2,256,512]{3,2,1,0:T(8,128)(2,1)} %constant_dynamic-update-slice_fusion.refs_5_), channel_id=1, source_target_pairs={{0,32},{8,40},{16,48},{24,56},{32,64},{40,72},{48,80},{56,88},{64,... | collective-permute-start | bytes 1572872 | tf_op jit(solution)/shard_map/ppermute | solution.py:36
  113.2 1.9 %collective-permute-start.13 = (bf16[1,2,256,512]{3,2,1,0:T(8,128)(2,1)}, bf16[1,2,256,512]{3,2,1,0:T(8,128)(2,1)}, u32[]{:S(2)}, u32[]{:S(2)}) collective-permute-start(bf16[1,2,256,512]{3,2,1,0:T(8,128)(2,1)} %constant_dynamic-update-slice_fusion.refs_5_), channel_id=1, source_target_pairs={{0,96},{8,104},{16,112},{24,120},{32,0},{40,8},{48,16},{56,24},{64... | collective-permute-start | bytes 1572872 | tf_op jit(solution)/shard_map/ppermute | solution.py:36
  115.3 1.1 pad_maximum_fusion.refs_5_
  118.9 2.2 %copy-done = bf16[1,2,256,4096]{3,2,1,0:T(8,128)(2,1)S(1)} copy-done((bf16[1,2,256,4096]{3,2,1,0:T(8,128)(2,1)S(1)}, bf16[1,2,256,4096]{3,2,1,0:T(8,128)(2,1)}, u32[]{:S(2)}) %copy-start) | copy-done | bytes 4194328
  121.1 1.0 copy-done.8
  122.1 1.0 copy-done.10
  123.1 1.0 copy-done.12
  124.2 1.0 copy-done.14
  125.2 4.8 %shard_map.28.refs_0_ = f32[1,2,256,512]{3,2,1,0:T(8,128)S(1)} custom-call(f32[8,32]{1,0:T(8,128)S(1)} %fusion.4.weights, s32[11]{0:T(128)S(1)} %stack.71.places, bf16[1,2,256,4096]{3,2,1,0:T(8,128)(2,1)S(1)} %copy-done, bf16[1,2,256,512]{3,2,1,0:T(8,128)(2,1)S(1)} %copy-done.2, bf16[1,2,256,512]{3,2,1,0:T(8,128)(2,1)S(1)} %collective-permute-done.refs_1_, ...), custom_call_target="tpu_custom_call" | custom-call | flops 2952790016 | bytes 11010048 | tf_op jit(solution)/shard_map/pallas_call | solution.py:78
  130.1 1.9 %collective-permute-done.12.refs_1_ = bf16[1,2,256,512]{3,2,1,0:T(8,128)(2,1)} collective-permute-done((bf16[1,2,256,512]{3,2,1,0:T(8,128)(2,1)}, bf16[1,2,256,512]{3,2,1,0:T(8,128)(2,1)}, u32[]{:S(2)}, u32[]{:S(2)}) %collective-permute-start.12) | collective-permute-done | bytes 524320 | tf_op jit(solution)/shard_map/ppermute | solution.py:36
  132.0 5.1 %collective-permute-done.13.refs_2_ = bf16[1,2,256,512]{3,2,1,0:T(8,128)(2,1)} collective-permute-done((bf16[1,2,256,512]{3,2,1,0:T(8,128)(2,1)}, bf16[1,2,256,512]{3,2,1,0:T(8,128)(2,1)}, u32[]{:S(2)}, u32[]{:S(2)}) %collective-permute-start.13) | collective-permute-done | bytes 524320 | tf_op jit(solution)/shard_map/ppermute | solution.py:36
  137.1 3.9 %shard_map.29 = f32[1,2,256,512]{3,2,1,0:T(8,128)} custom-call(f32[8,32]{1,0:T(8,128)S(1)} %fusion.4.weights, s32[5]{0:T(128)S(1)} %stack.59.places, bf16[1,2,256,4096]{3,2,1,0:T(8,128)(2,1)S(1)} %copy-done.1, f32[1,2,256,512]{3,2,1,0:T(8,128)S(1)} %shard_map.28.refs_0_, bf16[1,2,256,512]{3,2,1,0:T(8,128)(2,1)} %collective-permute-done.12.refs_1_, ...), custom_call_target="tpu_custom_call" | custom-call | flops 1342177280 | bytes 7864320 | tf_op jit(solution)/shard_map/pallas_call | solution.py:78
  (60 shorter events, 9.2 us)
Async XLA Ops:
  6.5 112.3 %copy-start.2 = (bf16[1,2,256,512]{3,2,1,0:T(8,128)(2,1)S(1)}, bf16[1,2,256,512]{3,2,1,0:T(8,128)(2,1)}, u32[]{:S(2)}) copy-start(bf16[1,2,256,512]{3,2,1,0:T(8,128)(2,1)} %refs_0_.1) | copy-start | bytes 1572868
  6.5 78.6 %copy-start.15 = (s32[2,4,3]{1,0,2:T(2,128)S(1)}, s32[2,4,3]{1,0,2:T(2,128)}, u32[]{:S(2)}) copy-start(s32[2,4,3]{1,0,2:T(2,128)} %param.3) | copy-start | bytes 292
  6.5 112.3 %all-gather.2.cloned.1.call-start = ((), (), s32[]{:S(2)}) async-start(), calls=%async_computation | async-start | bytes 4718592 | tf_op jit(solution)/shard_map/all_gather | solution.py:95
  7.3 29.2 %collective-permute-start = (bf16[1,2,256,512]{3,2,1,0:T(8,128)(2,1)}, bf16[1,2,256,512]{3,2,1,0:T(8,128)(2,1)S(1)}, u32[]{:S(2)}, u32[]{:S(2)}) collective-permute-start(bf16[1,2,256,512]{3,2,1,0:T(8,128)(2,1)} %refs_0_.1), channel_id=1, source_target_pairs={{0,32},{8,40},{16,48},{24,56},{32,64},{40,72},{48,80},{56,88},{64,... | collective-permute-start | bytes 1572872 | tf_op jit(solution)/shard_map/ppermute | solution.py:36
  11.8 28.0 %collective-permute-start.1 = (bf16[1,2,256,512]{3,2,1,0:T(8,128)(2,1)}, bf16[1,2,256,512]{3,2,1,0:T(8,128)(2,1)S(1)}, u32[]{:S(2)}, u32[]{:S(2)}) collective-permute-start(bf16[1,2,256,512]{3,2,1,0:T(8,128)(2,1)} %refs_0_.1), channel_id=1, source_target_pairs={{0,96},{8,104},{16,112},{24,120},{32,0},{40,8},{48,16},{56,24},{64... | collective-permute-start | bytes 1572872 | tf_op jit(solution)/shard_map/ppermute | solution.py:36
  36.5 15.1 %collective-permute-start.6 = (bf16[1,1,256,512]{3,2,1,0:T(8,128)(2,1)S(1)}, bf16[1,1,256,512]{3,2,1,0:T(8,128)(2,1)S(1)}, u32[]{:S(2)}, u32[]{:S(2)}) collective-permute-start(bf16[1,1,256,512]{3,2,1,0:T(8,128)(2,1)S(1)} %slice.38), channel_id=1, source_target_pairs={{0,32},{8,40},{16,48},{24,56},{32,64},{40,72},{48,80},{56,88},{64,... | collective-permute-start | bytes 786440 | tf_op jit(solution)/shard_map/ppermute | solution.py:36
  39.8 12.6 %collective-permute-start.7 = (bf16[1,1,256,512]{3,2,1,0:T(8,128)(2,1)S(1)}, bf16[1,1,256,512]{3,2,1,0:T(8,128)(2,1)S(1)}, u32[]{:S(2)}, u32[]{:S(2)}) collective-permute-start(bf16[1,1,256,512]{3,2,1,0:T(8,128)(2,1)S(1)} %slice.39), channel_id=1, source_target_pairs={{0,96},{8,104},{16,112},{24,120},{32,0},{40,8},{48,16},{56,24},{64... | collective-permute-start | bytes 786440 | tf_op jit(solution)/shard_map/ppermute | solution.py:36
  44.5 17.2 %collective-permute-start.2 = (bf16[1,2,256,512]{3,2,1,0:T(8,128)(2,1)}, bf16[1,2,256,512]{3,2,1,0:T(8,128)(2,1)S(1)}, u32[]{:S(2)}, u32[]{:S(2)}) collective-permute-start(bf16[1,2,256,512]{3,2,1,0:T(8,128)(2,1)} %refs_0_.1), channel_id=1, source_target_pairs={{0,8},{8,16},{16,24},{24,0},{32,40},{40,48},{48,56},{56,32},{64,72... | collective-permute-start | bytes 1572872 | tf_op jit(solution)/shard_map/ppermute | solution.py:36
  47.9 18.0 %collective-permute-start.3 = (bf16[1,2,256,512]{3,2,1,0:T(8,128)(2,1)}, bf16[1,2,256,512]{3,2,1,0:T(8,128)(2,1)S(1)}, u32[]{:S(2)}, u32[]{:S(2)}) collective-permute-start(bf16[1,2,256,512]{3,2,1,0:T(8,128)(2,1)} %refs_0_.1), channel_id=1, source_target_pairs={{0,24},{8,0},{16,8},{24,16},{32,56},{40,32},{48,40},{56,48},{64,88... | collective-permute-start | bytes 1572872 | tf_op jit(solution)/shard_map/ppermute | solution.py:36
  52.5 30.0 %copy-start.7 = (bf16[1,2,256,512]{3,2,1,0:T(8,128)(2,1)}, bf16[1,2,256,512]{3,2,1,0:T(8,128)(2,1)S(1)}, u32[]{:S(2)}) copy-start(bf16[1,2,256,512]{3,2,1,0:T(8,128)(2,1)S(1)} %constant_dynamic-update-slice_fusion.2.refs_6_) | copy-start | bytes 1572868
  52.5 23.6 %collective-permute-start.15 = (bf16[1,2,256,512]{3,2,1,0:T(8,128)(2,1)S(1)}, bf16[1,2,256,512]{3,2,1,0:T(8,128)(2,1)S(1)}, u32[]{:S(2)}, u32[]{:S(2)}) collective-permute-start(bf16[1,2,256,512]{3,2,1,0:T(8,128)(2,1)S(1)} %constant_dynamic-update-slice_fusion.2.refs_6_), channel_id=1, source_target_pairs={{0,24},{8,0},{16,8},{24,16},{32,56},{40,32},{48,40},{56,48},{64,88... | collective-permute-start | bytes 1572872 | tf_op jit(solution)/shard_map/ppermute | solution.py:36
  57.1 24.6 %collective-permute-start.14 = (bf16[1,2,256,512]{3,2,1,0:T(8,128)(2,1)S(1)}, bf16[1,2,256,512]{3,2,1,0:T(8,128)(2,1)S(1)}, u32[]{:S(2)}, u32[]{:S(2)}) collective-permute-start(bf16[1,2,256,512]{3,2,1,0:T(8,128)(2,1)S(1)} %constant_dynamic-update-slice_fusion.2.refs_6_), channel_id=1, source_target_pairs={{0,8},{8,16},{16,24},{24,0},{32,40},{40,48},{48,56},{56,32},{64,72... | collective-permute-start | bytes 1572872 | tf_op jit(solution)/shard_map/ppermute | solution.py:36
  59.1 38.8 %collective-permute-start.8 = (bf16[1,2,256,512]{3,2,1,0:T(8,128)(2,1)S(1)}, bf16[1,2,256,512]{3,2,1,0:T(8,128)(2,1)}, u32[]{:S(2)}, u32[]{:S(2)}) collective-permute-start(bf16[1,2,256,512]{3,2,1,0:T(8,128)(2,1)S(1)} %collective-permute-done.refs_1_), channel_id=1, source_target_pairs={{0,8},{8,16},{16,24},{24,0},{32,40},{40,48},{48,56},{56,32},{64,72... | collective-permute-start | bytes 1572872 | tf_op jit(solution)/shard_map/ppermute | solution.py:36
  62.5 29.5 %collective-permute-start.4 = (bf16[1,1,256,512]{3,2,1,0:T(8,128)(2,1)}, bf16[1,1,256,512]{3,2,1,0:T(8,128)(2,1)S(1)}, u32[]{:S(2)}, u32[]{:S(2)}) collective-permute-start(bf16[1,1,256,512]{3,2,1,0:T(8,128)(2,1)} %slice.36), channel_id=1, source_target_pairs={{0,8},{8,16},{16,24},{24,0},{32,40},{40,48},{48,56},{56,32},{64,72... | collective-permute-start | bytes 786440 | tf_op jit(solution)/shard_map/ppermute | solution.py:36
  66.6 27.3 %collective-permute-start.5 = (bf16[1,1,256,512]{3,2,1,0:T(8,128)(2,1)}, bf16[1,1,256,512]{3,2,1,0:T(8,128)(2,1)}, u32[]{:S(2)}, u32[]{:S(2)}) collective-permute-start(bf16[1,1,256,512]{3,2,1,0:T(8,128)(2,1)} %slice.37), channel_id=1, source_target_pairs={{0,24},{8,0},{16,8},{24,16},{32,56},{40,32},{48,40},{56,48},{64,88... | collective-permute-start | bytes 786440 | tf_op jit(solution)/shard_map/ppermute | solution.py:36
  76.1 39.1 %copy-start.3 = (bf16[1,2,256,512]{3,2,1,0:T(8,128)(2,1)}, bf16[1,2,256,512]{3,2,1,0:T(8,128)(2,1)S(1)}, u32[]{:S(2)}) copy-start(bf16[1,2,256,512]{3,2,1,0:T(8,128)(2,1)S(1)} %collective-permute-done.15.refs_4_) | copy-start | bytes 1572868
  76.9 26.5 %collective-permute-start.17 = (bf16[1,1,256,512]{3,2,1,0:T(8,128)(2,1)}, bf16[1,1,256,512]{3,2,1,0:T(8,128)(2,1)}, u32[]{:S(2)}, u32[]{:S(2)}) collective-permute-start(bf16[1,1,256,512]{3,2,1,0:T(8,128)(2,1)} %slice.41), channel_id=1, source_target_pairs={{0,24},{8,0},{16,8},{24,16},{32,56},{40,32},{48,40},{56,48},{64,88... | collective-permute-start | bytes 786440 | tf_op jit(solution)/shard_map/ppermute | solution.py:36
  83.2 30.0 %collective-permute-start.16 = (bf16[1,1,256,512]{3,2,1,0:T(8,128)(2,1)}, bf16[1,1,256,512]{3,2,1,0:T(8,128)(2,1)}, u32[]{:S(2)}, u32[]{:S(2)}) collective-permute-start(bf16[1,1,256,512]{3,2,1,0:T(8,128)(2,1)} %slice.40), channel_id=1, source_target_pairs={{0,8},{8,16},{16,24},{24,0},{32,40},{40,48},{48,56},{56,32},{64,72... | collective-permute-start | bytes 786440 | tf_op jit(solution)/shard_map/ppermute | solution.py:36
  92.0 24.4 %collective-permute-start.9 = (bf16[1,2,256,512]{3,2,1,0:T(8,128)(2,1)S(1)}, bf16[1,2,256,512]{3,2,1,0:T(8,128)(2,1)S(1)}, u32[]{:S(2)}, u32[]{:S(2)}) collective-permute-start(bf16[1,2,256,512]{3,2,1,0:T(8,128)(2,1)S(1)} %collective-permute-done.refs_1_), channel_id=1, source_target_pairs={{0,24},{8,0},{16,8},{24,16},{32,56},{40,32},{48,40},{56,48},{64,88... | collective-permute-start | bytes 1572872 | tf_op jit(solution)/shard_map/ppermute | solution.py:36
  93.9 23.3 %collective-permute-start.10 = (bf16[1,2,256,512]{3,2,1,0:T(8,128)(2,1)S(1)}, bf16[1,2,256,512]{3,2,1,0:T(8,128)(2,1)S(1)}, u32[]{:S(2)}, u32[]{:S(2)}) collective-permute-start(bf16[1,2,256,512]{3,2,1,0:T(8,128)(2,1)S(1)} %collective-permute-done.1.refs_2_), channel_id=1, source_target_pairs={{0,8},{8,16},{16,24},{24,0},{32,40},{40,48},{48,56},{56,32},{64,72... | collective-permute-start | bytes 1572872 | tf_op jit(solution)/shard_map/ppermute | solution.py:36
  97.8 20.2 %collective-permute-start.11 = (bf16[1,2,256,512]{3,2,1,0:T(8,128)(2,1)S(1)}, bf16[1,2,256,512]{3,2,1,0:T(8,128)(2,1)S(1)}, u32[]{:S(2)}, u32[]{:S(2)}) collective-permute-start(bf16[1,2,256,512]{3,2,1,0:T(8,128)(2,1)S(1)} %collective-permute-done.1.refs_2_), channel_id=1, source_target_pairs={{0,24},{8,0},{16,8},{24,16},{32,56},{40,32},{48,40},{56,48},{64,88... | collective-permute-start | bytes 1572872 | tf_op jit(solution)/shard_map/ppermute | solution.py:36
  103.4 28.6 %collective-permute-start.12 = (bf16[1,2,256,512]{3,2,1,0:T(8,128)(2,1)}, bf16[1,2,256,512]{3,2,1,0:T(8,128)(2,1)}, u32[]{:S(2)}, u32[]{:S(2)}) collective-permute-start(bf16[1,2,256,512]{3,2,1,0:T(8,128)(2,1)} %constant_dynamic-update-slice_fusion.refs_5_), channel_id=1, source_target_pairs={{0,32},{8,40},{16,48},{24,56},{32,64},{40,72},{48,80},{56,88},{64,... | collective-permute-start | bytes 1572872 | tf_op jit(solution)/shard_map/ppermute | solution.py:36
  113.2 23.8 %collective-permute-start.13 = (bf16[1,2,256,512]{3,2,1,0:T(8,128)(2,1)}, bf16[1,2,256,512]{3,2,1,0:T(8,128)(2,1)}, u32[]{:S(2)}, u32[]{:S(2)}) collective-permute-start(bf16[1,2,256,512]{3,2,1,0:T(8,128)(2,1)} %constant_dynamic-update-slice_fusion.refs_5_), channel_id=1, source_target_pairs={{0,96},{8,104},{16,112},{24,120},{32,0},{40,8},{48,16},{56,24},{64... | collective-permute-start | bytes 1572872 | tf_op jit(solution)/shard_map/ppermute | solution.py:36
  116.3 0.8 copy-start.9
  118.9 2.2 %copy-start = (bf16[1,2,256,4096]{3,2,1,0:T(8,128)(2,1)S(1)}, bf16[1,2,256,4096]{3,2,1,0:T(8,128)(2,1)}, u32[]{:S(2)}) copy-start(bf16[1,2,256,4096]{3,2,1,0:T(8,128)(2,1)} %all-gather.2.cloned.1.call-done.left) | copy-start | bytes 12582916
  121.1 1.0 copy-start.8
  122.1 1.0 copy-start.10
  123.1 1.0 copy-start.12
  124.2 1.0 copy-start.14
  125.2 11.9 %copy-start.1 = (bf16[1,2,256,4096]{3,2,1,0:T(8,128)(2,1)S(1)}, bf16[1,2,256,4096]{3,2,1,0:T(8,128)(2,1)}, u32[]{:S(2)}) copy-start(bf16[1,2,256,4096]{3,2,1,0:T(8,128)(2,1)} %all-gather.2.cloned.1.call-done.left) | copy-start | bytes 12582916
  125.2 11.9 %copy-start.4 = (bf16[1,2,256,512]{3,2,1,0:T(8,128)(2,1)S(1)}, bf16[1,2,256,512]{3,2,1,0:T(8,128)(2,1)}, u32[]{:S(2)}) copy-start(bf16[1,2,256,512]{3,2,1,0:T(8,128)(2,1)} %copy-done.3) | copy-start | bytes 1572868
  125.2 11.9 %copy-start.6 = (bf16[1,2,256,512]{3,2,1,0:T(8,128)(2,1)S(1)}, bf16[1,2,256,512]{3,2,1,0:T(8,128)(2,1)}, u32[]{:S(2)}) copy-start(bf16[1,2,256,512]{3,2,1,0:T(8,128)(2,1)} %copy-done.5) | copy-start | bytes 1572868
  (3 other events, 2.5 us)
Sparse Core Ops, SparseCore 0:
  9.4 55.0 all-gather.1

commit v2 on v1

v2 whole, which is shorter than its diff:
```python
import functools

import jax
import jax.numpy as jnp
from jax import lax
from jax.experimental import pallas as pl
from jax.experimental.pallas import tpu as pltpu
from jax.sharding import PartitionSpec as P

NB = 32
TILE = 128
SIDE = 4
ROWS = 256
COLS = 512
X_LINES = [[SIDE * y + x for x in range(SIDE)] for y in range(SIDE)]
Y_LINES = [[SIDE * y + x for y in range(SIDE)] for x in range(SIDE)]


def tile_weights(aperture):
    block_ids = jnp.arange(NB, dtype=jnp.int32)
    offset = block_ids[None, None, :] - aperture[..., 0:1]
    extent = aperture[..., 1:2]
    taper_width = aperture[..., 2:3]
    margin = jnp.minimum(offset, extent - 1 - offset)
    ramped = jnp.minimum(
        1.0, (margin + 1).astype(jnp.float32) / (taper_width + 1).astype(jnp.float32)
    )
    return jnp.where((offset >= 0) & (offset < extent), ramped, 0.0)


def shift(block, dy, dx):
    pairs = [
        (SIDE * y + x, SIDE * ((y + dy) % SIDE) + (x + dx) % SIDE)
        for y in range(SIDE)
        for x in range(SIDE)
    ]
    return lax.ppermute(block, "src", pairs)


def along(block, lines):
    copies = jnp.broadcast_to(block, (SIDE, *block.shape[1:]))
    return lax.all_to_all(copies, "src", 0, 0, tiled=True, axis_index_groups=lines)


def accumulate(steps, has_base, weights, source, left, *refs):
    out, base = refs[-1], refs[-2]
    y, x = source[0] // SIDE, lax.rem(source[0], SIDE)
    terms = []
    for array, index, dy, dx in steps:
        row, column = lax.rem(y + dy, SIDE), lax.rem(x + dx, SIDE)
        index = {"y": row, "x": column}.get(index, index)
        terms.append((row * SIDE + column, refs[array], index))
    for tile in range(COLS // TILE):
        cols = slice(tile * TILE, (tile + 1) * TILE)
        total = None
        for place, block, index in terms:
            parts = []
            for half in range(ROWS // TILE):
                lanes = pl.ds(pl.multiple_of(place * ROWS + half * TILE, TILE), TILE)
                rows = []
                for part in range(2):
                    for a in range(2):
                        value = left[0, part, a * TILE : (a + 1) * TILE, lanes]
                        weight = weights[a * 4 + tile, 2 * place + half]
                        rows.append((value.astype(jnp.float32) * weight).astype(jnp.bfloat16))
                parts.append(jnp.concatenate(rows, axis=0))
            scaled = jnp.concatenate(parts, axis=1)
            right = jnp.concatenate([block[index, 0, :, cols], block[index, 1, :, cols]], axis=1)
            product = jnp.dot(scaled, right, preferred_element_type=jnp.float32)
            total = product if total is None else total + product
        real = total[:ROWS, :TILE] - total[ROWS:, TILE:]
        imag = total[:ROWS, TILE:] + total[ROWS:, :TILE]
        if has_base:
            real, imag = real + base[0, 0, :, cols], imag + base[0, 1, :, cols]
        out[0, 0, :, cols] = real
        out[0, 1, :, cols] = imag


def add_blocks(weights, source, left, arrays, steps, base=None):
    extra = [] if base is None else [base]
    smem = pl.BlockSpec(memory_space=pltpu.SMEM)
    vmem = pl.BlockSpec(memory_space=pltpu.VMEM)
    return pl.pallas_call(
        functools.partial(accumulate, steps, base is not None),
        out_shape=jax.ShapeDtypeStruct((1, 2, ROWS, COLS), jnp.float32),
        in_specs=[smem, smem] + [vmem] * (1 + len(arrays) + len(extra)),
        out_specs=vmem,
        compiler_params=pltpu.CompilerParams(vmem_limit_bytes=20 << 20),
        cost_estimate=pl.CostEstimate(
            flops=len(steps) * 6 * 4 * ROWS * ROWS * COLS,
            bytes_accessed=len(steps) * (1 << 19) + (5 << 20),
            transcendentals=0,
        ),
    )(weights, source, left, *arrays, *extra)


def shards(recorded, aperture):
    weights = tile_weights(aperture).reshape(8, NB)
    source = lax.axis_index("src")
    x = source % SIDE
    y = source // SIDE
    left = lax.all_gather(recorded, "rcv", axis=3, tiled=True)
    above, below = shift(recorded, 1, 0), shift(recorded, -1, 0)
    before, after = shift(recorded, 0, 1), shift(recorded, 0, -1)
    opposite = shift(recorded, 0, 2)
    across = [shift(above[:, :1], 1, 0), shift(below[:, 1:], -1, 0)]
    *across, before, after, opposite = lax.optimization_barrier((*across, before, after, opposite))
    pair = jnp.concatenate([above, below], axis=0)
    pair_left, pair_right = shift(pair, 0, 1), shift(pair, 0, -1)
    across_line = along(jnp.concatenate(across, axis=1), X_LINES)
    opposite_above, opposite_below = shift(opposite, 1, 0), shift(opposite, -1, 0)

    early = [recorded, above, below, before, after, opposite, pair_left, pair_right]
    steps = [(0, 0, 0, 0), (1, 0, 3, 0), (2, 0, 1, 0), (3, 0, 0, 3), (4, 0, 0, 1), (5, 0, 0, 2)]
    steps += [(6, 0, 3, 3), (6, 1, 1, 3), (7, 0, 3, 1), (7, 1, 1, 1)]
    source = source.reshape(1)
    total = add_blocks(weights, source, left, early, steps)
    late = [opposite_above, opposite_below, across_line]
    steps = [(0, 0, 3, 2), (1, 0, 1, 2)] + [(2, "x", 2, i) for i in range(SIDE)]
    return add_blocks(weights, source, left, late, steps, total)


def solution(mesh):
    in_specs = (P("grp", None, "src", "rcv"), P(("grp", "src"), "rcv", None))
    out_specs = P("grp", None, "src", "rcv")
    return jax.shard_map(shards, mesh=mesh, in_specs=in_specs, out_specs=out_specs, check_vma=False)
```

time: 149 us -> 117 us (0.79)
  the two profiles are of different devices: /device:TPU:456 before, /device:TPU:384 now
where the time goes in v2:
time: 117 us
  starting transfers between devices  48.8 us (42%)
  waiting for transfers between devices  30.4 us (26%)
  local copies, waits for them, and re-layouts  14.9 us (13%)
  between operations  13.6 us (12%)
  Pallas kernels  8.66 us (7%)
    ppermute x11, starting transfers between devices, shift(): return lax.ppermute(block, 'src', pairs)  44.5 us
    ppermute x11, waiting for transfers between devices, shift(): return lax.ppermute(block, 'src', pairs)  21.5 us
    unnamed x21, local copies, waits for them, and re-layouts  12.2 us
    pallas_call x2, Pallas kernels, add_blocks(): pl.pallas_call(functools.partial(accumulate, steps, base is not None), ou...  8.66 us
    all_to_all x1, waiting for transfers between devices, along(): lax.all_to_all(copies, 'src', 0, 0, tiled=True, axis_index_groups=lines)  8.22 us
    all_to_all x1, starting transfers between devices, along(): lax.all_to_all(copies, 'src', 0, 0, tiled=True, axis_index_groups=lines)  4.32 us
  transfers between devices with their start and end apart: 13, of which 7 were waited for; matrix products, arithmetic and copies ran while one was open for 3% of the time, Pallas kernels for 4%

profile of v2, /device:TPU:384, one launch (start us, length us, event | category | flops | bytes accessed | tf_op | source)
XLA Modules:
  0.0 116.5 jit_solution(18119052591266296082)
XLA Ops:
  7.3 4.5 %collective-permute-start = (bf16[1,2,256,512]{3,2,1,0:T(8,128)(2,1)}, bf16[1,2,256,512]{3,2,1,0:T(8,128)(2,1)S(1)}, u32[]{:S(2)}, u32[]{:S(2)}) collective-permute-start(bf16[1,2,256,512]{3,2,1,0:T(8,128)(2,1)} %refs_0_.1), channel_id=1, source_target_pairs={{0,32},{8,40},{16,48},{24,56},{32,64},{40,72},{48,80},{56,88},{64,... | collective-permute-start | bytes 1572872 | tf_op jit(solution)/shard_map/ppermute | solution.py:37
  11.8 3.6 %collective-permute-start.2 = (bf16[1,2,256,512]{3,2,1,0:T(8,128)(2,1)}, bf16[1,2,256,512]{3,2,1,0:T(8,128)(2,1)S(1)}, u32[]{:S(2)}, u32[]{:S(2)}) collective-permute-start(bf16[1,2,256,512]{3,2,1,0:T(8,128)(2,1)} %refs_0_.1), channel_id=1, source_target_pairs={{0,96},{8,104},{16,112},{24,120},{32,0},{40,8},{48,16},{56,24},{64... | collective-permute-start | bytes 1572872 | tf_op jit(solution)/shard_map/ppermute | solution.py:37
  15.4 3.4 %collective-permute-start.4 = (bf16[1,2,256,512]{3,2,1,0:T(8,128)(2,1)}, bf16[1,2,256,512]{3,2,1,0:T(8,128)(2,1)S(1)}, u32[]{:S(2)}, u32[]{:S(2)}) collective-permute-start(bf16[1,2,256,512]{3,2,1,0:T(8,128)(2,1)} %refs_0_.1), channel_id=1, source_target_pairs={{0,8},{8,16},{16,24},{24,0},{32,40},{40,48},{48,56},{56,32},{64,72... | collective-permute-start | bytes 1572872 | tf_op jit(solution)/shard_map/ppermute | solution.py:37
  18.8 3.7 %collective-permute-start.5 = (bf16[1,2,256,512]{3,2,1,0:T(8,128)(2,1)}, bf16[1,2,256,512]{3,2,1,0:T(8,128)(2,1)S(1)}, u32[]{:S(2)}, u32[]{:S(2)}) collective-permute-start(bf16[1,2,256,512]{3,2,1,0:T(8,128)(2,1)} %refs_0_.1), channel_id=1, source_target_pairs={{0,24},{8,0},{16,8},{24,16},{32,56},{40,32},{48,40},{56,48},{64,88... | collective-permute-start | bytes 1572872 | tf_op jit(solution)/shard_map/ppermute | solution.py:37
  22.4 3.7 %collective-permute-start.6 = (bf16[1,2,256,512]{3,2,1,0:T(8,128)(2,1)}, bf16[1,2,256,512]{3,2,1,0:T(8,128)(2,1)}, u32[]{:S(2)}, u32[]{:S(2)}) collective-permute-start(bf16[1,2,256,512]{3,2,1,0:T(8,128)(2,1)} %refs_0_.1), channel_id=1, source_target_pairs={{0,16},{8,24},{16,0},{24,8},{32,48},{40,56},{48,32},{56,40},{64,80... | collective-permute-start | bytes 1572872 | tf_op jit(solution)/shard_map/ppermute | solution.py:37
  26.2 6.7 %collective-permute-done.refs_1_ = bf16[1,2,256,512]{3,2,1,0:T(8,128)(2,1)S(1)} collective-permute-done((bf16[1,2,256,512]{3,2,1,0:T(8,128)(2,1)}, bf16[1,2,256,512]{3,2,1,0:T(8,128)(2,1)S(1)}, u32[]{:S(2)}, u32[]{:S(2)}) %collective-permute-start) | collective-permute-done | bytes 524320 | tf_op jit(solution)/shard_map/ppermute | solution.py:37
  32.9 7.2 %collective-permute-start.1 = (bf16[1,1,256,512]{3,2,1,0:T(8,128)(2,1)S(1)}, bf16[1,1,256,512]{3,2,1,0:T(8,128)(2,1)S(1)}, u32[]{:S(2)}, u32[]{:S(2)}) collective-permute-start(bf16[1,1,256,512]{3,2,1,0:T(8,128)(2,1)S(1)} %slice.20), channel_id=1, source_target_pairs={{0,32},{8,40},{16,48},{24,56},{32,64},{40,72},{48,80},{56,88},{64,... | collective-permute-start | bytes 786440 | tf_op jit(solution)/shard_map/ppermute | solution.py:37
  40.6 3.9 %collective-permute-start.3 = (bf16[1,1,256,512]{3,2,1,0:T(8,128)(2,1)S(1)}, bf16[1,1,256,512]{3,2,1,0:T(8,128)(2,1)S(1)}, u32[]{:S(2)}, u32[]{:S(2)}) collective-permute-start(bf16[1,1,256,512]{3,2,1,0:T(8,128)(2,1)S(1)} %slice.21), channel_id=1, source_target_pairs={{0,96},{8,104},{16,112},{24,120},{32,0},{40,8},{48,16},{56,24},{64... | collective-permute-start | bytes 786440 | tf_op jit(solution)/shard_map/ppermute | solution.py:37
  44.5 0.8 constant_dynamic-update-slice_fusion.1
  45.3 0.8 constant_dynamic-update-slice_fusion
  46.2 0.8 copy-done.3
  47.0 4.7 %collective-permute-start.10 = (bf16[2,2,256,512]{3,2,1,0:T(8,128)(2,1)}, bf16[2,2,256,512]{3,2,1,0:T(8,128)(2,1)}, u32[]{:S(2)}, u32[]{:S(2)}) collective-permute-start(bf16[2,2,256,512]{3,2,1,0:T(8,128)(2,1)} %constant_dynamic-update-slice_fusion), channel_id=1, source_target_pairs={{0,24},{8,0},{16,8},{24,16},{32,56},{40,32},{48,40},{56,48},{64,88... | collective-permute-start | bytes 3145736 | tf_op jit(solution)/shard_map/ppermute | solution.py:37
  51.7 0.8 copy-done.5
  52.5 1.9 %collective-permute-start.9 = (bf16[2,2,256,512]{3,2,1,0:T(8,128)(2,1)}, bf16[2,2,256,512]{3,2,1,0:T(8,128)(2,1)}, u32[]{:S(2)}, u32[]{:S(2)}) collective-permute-start(bf16[2,2,256,512]{3,2,1,0:T(8,128)(2,1)} %constant_dynamic-update-slice_fusion), channel_id=1, source_target_pairs={{0,8},{8,16},{16,24},{24,0},{32,40},{40,48},{48,56},{56,32},{64,72... | collective-permute-start | bytes 3145736 | tf_op jit(solution)/shard_map/ppermute | solution.py:37
  54.4 3.1 %collective-permute-done.3 = bf16[1,1,256,512]{3,2,1,0:T(8,128)(2,1)S(1)} collective-permute-done((bf16[1,1,256,512]{3,2,1,0:T(8,128)(2,1)S(1)}, bf16[1,1,256,512]{3,2,1,0:T(8,128)(2,1)S(1)}, u32[]{:S(2)}, u32[]{:S(2)}) %collective-permute-start.3) | collective-permute-done | bytes 262176 | tf_op jit(solution)/shard_map/ppermute | solution.py:37
  57.6 1.5 %broadcast_in_dim.14 = bf16[4,2,256,512]{3,2,1,0:T(8,128)(2,1)} broadcast(bf16[2,256,512]{2,1,0:T(8,128)(2,1)S(1)} %maximum_bitcast_fusion), dimensions={1,2,3} | broadcast | bytes 2621440 | tf_op jit(solution)/shard_map/broadcast_in_dim | solution.py:41
  59.2 4.3 %all-to-all-start = ((bf16[4,2,256,512]{3,2,1,0:T(8,128)(2,1)}), bf16[4,2,256,512]{3,2,1,0:T(8,128)(2,1)S(1)}, u32[]{:S(2)}, u32[]{:S(2)}) async-start(bf16[4,2,256,512]{3,2,1,0:T(8,128)(2,1)} %broadcast_in_dim.14), calls=%async_computation | async-start | bytes 4194304 | tf_op jit(solution)/shard_map/all_to_all | solution.py:42
  63.9 4.0 %collective-permute-start.7 = (bf16[1,2,256,512]{3,2,1,0:T(8,128)(2,1)}, bf16[1,2,256,512]{3,2,1,0:T(8,128)(2,1)}, u32[]{:S(2)}, u32[]{:S(2)}) collective-permute-start(bf16[1,2,256,512]{3,2,1,0:T(8,128)(2,1)} %collective-permute-done.6.refs_5_), channel_id=1, source_target_pairs={{0,32},{8,40},{16,48},{24,56},{32,64},{40,72},{48,80},{56,88},{64,... | collective-permute-start | bytes 1572872 | tf_op jit(solution)/shard_map/ppermute | solution.py:37
  67.9 4.0 %collective-permute-start.8 = (bf16[1,2,256,512]{3,2,1,0:T(8,128)(2,1)}, bf16[1,2,256,512]{3,2,1,0:T(8,128)(2,1)}, u32[]{:S(2)}, u32[]{:S(2)}) collective-permute-start(bf16[1,2,256,512]{3,2,1,0:T(8,128)(2,1)} %collective-permute-done.6.refs_5_), channel_id=1, source_target_pairs={{0,96},{8,104},{16,112},{24,120},{32,0},{40,8},{48,16},{56,24},{64... | collective-permute-start | bytes 1572872 | tf_op jit(solution)/shard_map/ppermute | solution.py:37
  71.9 3.7 %collective-permute-done.10.refs_7_ = bf16[2,2,256,512]{3,2,1,0:T(8,128)(2,1)} collective-permute-done((bf16[2,2,256,512]{3,2,1,0:T(8,128)(2,1)}, bf16[2,2,256,512]{3,2,1,0:T(8,128)(2,1)}, u32[]{:S(2)}, u32[]{:S(2)}) %collective-permute-start.10) | collective-permute-done | bytes 1048608 | tf_op jit(solution)/shard_map/ppermute | solution.py:37
  75.6 6.4 %collective-permute-done.9.refs_6_ = bf16[2,2,256,512]{3,2,1,0:T(8,128)(2,1)} collective-permute-done((bf16[2,2,256,512]{3,2,1,0:T(8,128)(2,1)}, bf16[2,2,256,512]{3,2,1,0:T(8,128)(2,1)}, u32[]{:S(2)}, u32[]{:S(2)}) %collective-permute-start.9) | collective-permute-done | bytes 1048608 | tf_op jit(solution)/shard_map/ppermute | solution.py:37
  82.0 1.0 copy-done
  83.0 2.2 %copy-done.1 = bf16[1,2,256,4096]{3,2,1,0:T(8,128)(2,1)S(1)} copy-done((bf16[1,2,256,4096]{3,2,1,0:T(8,128)(2,1)S(1)}, bf16[1,2,256,4096]{3,2,1,0:T(8,128)(2,1)}, u32[]{:S(2)}) %copy-start.1) | copy-done | bytes 4194328
  85.2 1.0 copy-done.4
  86.3 1.0 copy-done.6
  87.3 4.6 %shard_map.28.refs_3_ = f32[1,2,256,512]{3,2,1,0:T(8,128)S(1)} custom-call(f32[8,32]{1,0:T(8,128)S(1)} %fusion.4.weights, s32[1]{0:T(128)} %bitcast.source, bf16[1,2,256,4096]{3,2,1,0:T(8,128)(2,1)S(1)} %copy-done.1, bf16[1,2,256,512]{3,2,1,0:T(8,128)(2,1)S(1)} %copy-done, bf16[1,2,256,512]{3,2,1,0:T(8,128)(2,1)S(1)} %collective-permute-done.refs_1_, ...), custom_call_target="tpu_custom_call" | custom-call | flops 8053063680 | bytes 10485760 | tf_op jit(solution)/shard_map/pallas_call | solution.py:83
  92.0 1.0 copy-done.7
  92.9 1.1 collective-permute-done.8.refs_1_
  94.1 8.2 %all-to-all-done.refs_2_ = bf16[4,2,256,512]{3,2,1,0:T(8,128)(2,1)S(1)} async-done(((bf16[4,2,256,512]{3,2,1,0:T(8,128)(2,1)}), bf16[4,2,256,512]{3,2,1,0:T(8,128)(2,1)S(1)}, u32[]{:S(2)}, u32[]{:S(2)}) %all-to-all-start) | async-done | bytes 2097184 | tf_op jit(solution)/shard_map/all_to_all | solution.py:42
  102.3 2.2 %copy-done.2 = bf16[1,2,256,4096]{3,2,1,0:T(8,128)(2,1)S(1)} copy-done((bf16[1,2,256,4096]{3,2,1,0:T(8,128)(2,1)S(1)}, bf16[1,2,256,4096]{3,2,1,0:T(8,128)(2,1)}, u32[]{:S(2)}) %copy-start.2) | copy-done | bytes 4194328
  104.5 1.2 %copy-done.8 = f32[1,2,256,512]{3,2,1,0:T(8,128)S(1)} copy-done((f32[1,2,256,512]{3,2,1,0:T(8,128)S(1)}, f32[1,2,256,512]{3,2,1,0:T(8,128)}, u32[]{:S(2)}) %copy-start.8) | copy-done | bytes 1048600
  105.7 4.0 %shard_map.29 = f32[1,2,256,512]{3,2,1,0:T(8,128)} custom-call(f32[8,32]{1,0:T(8,128)S(1)} %fusion.4.weights, s32[1]{0:T(128)} %bitcast.source, bf16[1,2,256,4096]{3,2,1,0:T(8,128)(2,1)S(1)} %copy-done.2, bf16[1,2,256,512]{3,2,1,0:T(8,128)(2,1)} %collective-permute-done.7.refs_0_, bf16[1,2,256,512]{3,2,1,0:T(8,128)(2,1)} %collective-permute-done.8.refs_1_, ...), custom_call_target="tpu_custom_call" | custom-call | flops 4831838208 | bytes 8388608 | tf_op jit(solution)/shard_map/pallas_call | solution.py:83
  (29 shorter events, 1.7 us)
Async XLA Ops:
  6.5 75.5 %all-gather.2.cloned.1.call-start = ((), (), s32[]{:S(2)}) async-start(), calls=%async_computation.1 | async-start | bytes 4718592 | tf_op jit(solution)/shard_map/all_gather | solution.py:102
  7.3 25.6 %collective-permute-start = (bf16[1,2,256,512]{3,2,1,0:T(8,128)(2,1)}, bf16[1,2,256,512]{3,2,1,0:T(8,128)(2,1)S(1)}, u32[]{:S(2)}, u32[]{:S(2)}) collective-permute-start(bf16[1,2,256,512]{3,2,1,0:T(8,128)(2,1)} %refs_0_.1), channel_id=1, source_target_pairs={{0,32},{8,40},{16,48},{24,56},{32,64},{40,72},{48,80},{56,88},{64,... | collective-permute-start | bytes 1572872 | tf_op jit(solution)/shard_map/ppermute | solution.py:37
  11.8 28.8 %collective-permute-start.2 = (bf16[1,2,256,512]{3,2,1,0:T(8,128)(2,1)}, bf16[1,2,256,512]{3,2,1,0:T(8,128)(2,1)S(1)}, u32[]{:S(2)}, u32[]{:S(2)}) collective-permute-start(bf16[1,2,256,512]{3,2,1,0:T(8,128)(2,1)} %refs_0_.1), channel_id=1, source_target_pairs={{0,96},{8,104},{16,112},{24,120},{32,0},{40,8},{48,16},{56,24},{64... | collective-permute-start | bytes 1572872 | tf_op jit(solution)/shard_map/ppermute | solution.py:37
  15.4 30.8 %collective-permute-start.4 = (bf16[1,2,256,512]{3,2,1,0:T(8,128)(2,1)}, bf16[1,2,256,512]{3,2,1,0:T(8,128)(2,1)S(1)}, u32[]{:S(2)}, u32[]{:S(2)}) collective-permute-start(bf16[1,2,256,512]{3,2,1,0:T(8,128)(2,1)} %refs_0_.1), channel_id=1, source_target_pairs={{0,8},{8,16},{16,24},{24,0},{32,40},{40,48},{48,56},{56,32},{64,72... | collective-permute-start | bytes 1572872 | tf_op jit(solution)/shard_map/ppermute | solution.py:37
  18.8 32.9 %collective-permute-start.5 = (bf16[1,2,256,512]{3,2,1,0:T(8,128)(2,1)}, bf16[1,2,256,512]{3,2,1,0:T(8,128)(2,1)S(1)}, u32[]{:S(2)}, u32[]{:S(2)}) collective-permute-start(bf16[1,2,256,512]{3,2,1,0:T(8,128)(2,1)} %refs_0_.1), channel_id=1, source_target_pairs={{0,24},{8,0},{16,8},{24,16},{32,56},{40,32},{48,40},{56,48},{64,88... | collective-permute-start | bytes 1572872 | tf_op jit(solution)/shard_map/ppermute | solution.py:37
  22.4 32.0 %collective-permute-start.6 = (bf16[1,2,256,512]{3,2,1,0:T(8,128)(2,1)}, bf16[1,2,256,512]{3,2,1,0:T(8,128)(2,1)}, u32[]{:S(2)}, u32[]{:S(2)}) collective-permute-start(bf16[1,2,256,512]{3,2,1,0:T(8,128)(2,1)} %refs_0_.1), channel_id=1, source_target_pairs={{0,16},{8,24},{16,0},{24,8},{32,48},{40,56},{48,32},{56,40},{64,80... | collective-permute-start | bytes 1572872 | tf_op jit(solution)/shard_map/ppermute | solution.py:37
  32.9 21.6 %collective-permute-start.1 = (bf16[1,1,256,512]{3,2,1,0:T(8,128)(2,1)S(1)}, bf16[1,1,256,512]{3,2,1,0:T(8,128)(2,1)S(1)}, u32[]{:S(2)}, u32[]{:S(2)}) collective-permute-start(bf16[1,1,256,512]{3,2,1,0:T(8,128)(2,1)S(1)} %slice.20), channel_id=1, source_target_pairs={{0,32},{8,40},{16,48},{24,56},{32,64},{40,72},{48,80},{56,88},{64,... | collective-permute-start | bytes 786440 | tf_op jit(solution)/shard_map/ppermute | solution.py:37
  40.6 17.0 %collective-permute-start.3 = (bf16[1,1,256,512]{3,2,1,0:T(8,128)(2,1)S(1)}, bf16[1,1,256,512]{3,2,1,0:T(8,128)(2,1)S(1)}, u32[]{:S(2)}, u32[]{:S(2)}) collective-permute-start(bf16[1,1,256,512]{3,2,1,0:T(8,128)(2,1)S(1)} %slice.21), channel_id=1, source_target_pairs={{0,96},{8,104},{16,112},{24,120},{32,0},{40,8},{48,16},{56,24},{64... | collective-permute-start | bytes 786440 | tf_op jit(solution)/shard_map/ppermute | solution.py:37
  46.2 0.8 copy-start.3
  47.0 28.6 %collective-permute-start.10 = (bf16[2,2,256,512]{3,2,1,0:T(8,128)(2,1)}, bf16[2,2,256,512]{3,2,1,0:T(8,128)(2,1)}, u32[]{:S(2)}, u32[]{:S(2)}) collective-permute-start(bf16[2,2,256,512]{3,2,1,0:T(8,128)(2,1)} %constant_dynamic-update-slice_fusion), channel_id=1, source_target_pairs={{0,24},{8,0},{16,8},{24,16},{32,56},{40,32},{48,40},{56,48},{64,88... | collective-permute-start | bytes 3145736 | tf_op jit(solution)/shard_map/ppermute | solution.py:37
  51.7 0.8 copy-start.5
  52.5 29.5 %collective-permute-start.9 = (bf16[2,2,256,512]{3,2,1,0:T(8,128)(2,1)}, bf16[2,2,256,512]{3,2,1,0:T(8,128)(2,1)}, u32[]{:S(2)}, u32[]{:S(2)}) collective-permute-start(bf16[2,2,256,512]{3,2,1,0:T(8,128)(2,1)} %constant_dynamic-update-slice_fusion), channel_id=1, source_target_pairs={{0,8},{8,16},{16,24},{24,0},{32,40},{40,48},{48,56},{56,32},{64,72... | collective-permute-start | bytes 3145736 | tf_op jit(solution)/shard_map/ppermute | solution.py:37
  59.2 4.3 %copy-start.9 = (s32[2,4,3]{1,0,2:T(2,128)S(1)}, s32[2,4,3]{1,0,2:T(2,128)}, u32[]{:S(2)}) copy-start(s32[2,4,3]{1,0,2:T(2,128)} %param.3) | copy-start | bytes 292
  59.2 43.1 %all-to-all-start = ((bf16[4,2,256,512]{3,2,1,0:T(8,128)(2,1)}), bf16[4,2,256,512]{3,2,1,0:T(8,128)(2,1)S(1)}, u32[]{:S(2)}, u32[]{:S(2)}) async-start(bf16[4,2,256,512]{3,2,1,0:T(8,128)(2,1)} %broadcast_in_dim.14), calls=%async_computation | async-start | bytes 4194304 | tf_op jit(solution)/shard_map/all_to_all | solution.py:42
  63.9 29.0 %collective-permute-start.7 = (bf16[1,2,256,512]{3,2,1,0:T(8,128)(2,1)}, bf16[1,2,256,512]{3,2,1,0:T(8,128)(2,1)}, u32[]{:S(2)}, u32[]{:S(2)}) collective-permute-start(bf16[1,2,256,512]{3,2,1,0:T(8,128)(2,1)} %collective-permute-done.6.refs_5_), channel_id=1, source_target_pairs={{0,32},{8,40},{16,48},{24,56},{32,64},{40,72},{48,80},{56,88},{64,... | collective-permute-start | bytes 1572872 | tf_op jit(solution)/shard_map/ppermute | solution.py:37
  67.9 26.1 %collective-permute-start.8 = (bf16[1,2,256,512]{3,2,1,0:T(8,128)(2,1)}, bf16[1,2,256,512]{3,2,1,0:T(8,128)(2,1)}, u32[]{:S(2)}, u32[]{:S(2)}) collective-permute-start(bf16[1,2,256,512]{3,2,1,0:T(8,128)(2,1)} %collective-permute-done.6.refs_5_), channel_id=1, source_target_pairs={{0,96},{8,104},{16,112},{24,120},{32,0},{40,8},{48,16},{56,24},{64... | collective-permute-start | bytes 1572872 | tf_op jit(solution)/shard_map/ppermute | solution.py:37
  82.0 1.0 copy-start
  83.0 2.2 %copy-start.1 = (bf16[1,2,256,4096]{3,2,1,0:T(8,128)(2,1)S(1)}, bf16[1,2,256,4096]{3,2,1,0:T(8,128)(2,1)}, u32[]{:S(2)}) copy-start(bf16[1,2,256,4096]{3,2,1,0:T(8,128)(2,1)} %all-gather.2.cloned.1.call-done.left) | copy-start | bytes 12582916
  85.2 1.0 copy-start.4
  86.3 1.0 copy-start.6
  92.0 1.0 copy-start.7
  102.3 2.2 %copy-start.2 = (bf16[1,2,256,4096]{3,2,1,0:T(8,128)(2,1)S(1)}, bf16[1,2,256,4096]{3,2,1,0:T(8,128)(2,1)}, u32[]{:S(2)}) copy-start(bf16[1,2,256,4096]{3,2,1,0:T(8,128)(2,1)} %all-gather.2.cloned.1.call-done.left) | copy-start | bytes 12582916
  104.5 1.2 %copy-start.8 = (f32[1,2,256,512]{3,2,1,0:T(8,128)S(1)}, f32[1,2,256,512]{3,2,1,0:T(8,128)}, u32[]{:S(2)}) copy-start(f32[1,2,256,512]{3,2,1,0:T(8,128)} %copy-done.7) | copy-start | bytes 3145732
Sparse Core Ops, SparseCore 0:
  9.4 55.8 all-gather.1

commit v3 on v2

v3 whole, which is shorter than its diff:
```python
import functools

import jax
import jax.numpy as jnp
from jax import lax
from jax.experimental import pallas as pl
from jax.experimental.pallas import tpu as pltpu
from jax.sharding import PartitionSpec as P

NB = 32
TILE = 128
SIDE = 4
ROWS = 256
COLS = 512
X_LINES = [[SIDE * y + x for x in range(SIDE)] for y in range(SIDE)]
Y_LINES = [[SIDE * y + x for y in range(SIDE)] for x in range(SIDE)]


def tile_weights(aperture):
    block_ids = jnp.arange(NB, dtype=jnp.int32)
    offset = block_ids[None, None, :] - aperture[..., 0:1]
    extent = aperture[..., 1:2]
    taper_width = aperture[..., 2:3]
    margin = jnp.minimum(offset, extent - 1 - offset)
    ramped = jnp.minimum(
        1.0, (margin + 1).astype(jnp.float32) / (taper_width + 1).astype(jnp.float32)
    )
    return jnp.where((offset >= 0) & (offset < extent), ramped, 0.0)


def shift(block, dy, dx):
    pairs = [
        (SIDE * y + x, SIDE * ((y + dy) % SIDE) + (x + dx) % SIDE)
        for y in range(SIDE)
        for x in range(SIDE)
    ]
    return lax.ppermute(block, "src", pairs)


def along(block, lines):
    copies = jnp.broadcast_to(block, (SIDE, *block.shape[1:]))
    return lax.all_to_all(copies, "src", 0, 0, tiled=True, axis_index_groups=lines)


def locate(source, steps):
    y, x = source[0] // SIDE, lax.rem(source[0], SIDE)
    found = []
    for _, index, dy, dx in steps:
        row, column = lax.rem(y + dy, SIDE), lax.rem(x + dx, SIDE)
        found.append((row * SIDE + column, {"y": row, "x": column}.get(index, index)))
    return found


def sum_tile(weights, tile, places, lefts, rights):
    cols = slice(tile * TILE, (tile + 1) * TILE)
    total = None
    for place, left, right in zip(places, lefts, rights):
        parts = []
        for half in range(ROWS // TILE):
            lanes = slice(half * TILE, (half + 1) * TILE)
            rows = []
            for part in range(2):
                for a in range(2):
                    value = left[part, a * TILE : (a + 1) * TILE, lanes]
                    weight = weights[a * 4 + tile, 2 * place + half]
                    rows.append((value.astype(jnp.float32) * weight).astype(jnp.bfloat16))
            parts.append(jnp.concatenate(rows, axis=0))
        scaled = jnp.concatenate(parts, axis=1)
        both = jnp.concatenate([right[0, :, cols], right[1, :, cols]], axis=1)
        product = jnp.dot(scaled, both, preferred_element_type=jnp.float32)
        total = product if total is None else total + product
    real = total[:ROWS, :TILE] - total[ROWS:, TILE:]
    imag = total[:ROWS, TILE:] + total[ROWS:, :TILE]
    return cols, real, imag


def sum_early(steps, late, group, weights, source, left, *refs):
    *arrays, out, late_left, lefts, rights, left_done, right_done, late_done = refs

    def columns(place):
        return left.at[0, :, :, pl.ds(pl.multiple_of(place * ROWS, ROWS), ROWS)]

    places, copies = [], []
    for number, (place, index) in enumerate(locate(source, steps)):
        block = arrays[steps[number][0]].at[index]
        pair = (
            pltpu.make_async_copy(columns(place), lefts.at[number], left_done.at[number]),
            pltpu.make_async_copy(block, rights.at[number], right_done.at[number]),
        )
        for copy in pair:
            copy.start()
        places.append(place)
        copies.append(pair)
    kept = [
        pltpu.make_async_copy(columns(place), late_left.at[number], late_done.at[number])
        for number, (place, _) in enumerate(locate(source, late))
    ]
    for copy in kept:
        copy.start()
    for first in range(0, len(steps), group):
        numbers = range(first, min(first + group, len(steps)))
        for number in numbers:
            for copy in copies[number]:
                copy.wait()
        for tile in range(COLS // TILE):
            cols, real, imag = sum_tile(
                weights,
                tile,
                [places[n] for n in numbers],
                [lefts.at[n] for n in numbers],
                [rights.at[n] for n in numbers],
            )
            if first > 0:
                real, imag = real + out[0, 0, :, cols], imag + out[0, 1, :, cols]
            out[0, 0, :, cols] = real
            out[0, 1, :, cols] = imag
    for copy in kept:
        copy.wait()


def sum_late(steps, group, weights, source, base, late_left, *refs):
    *arrays, out, sum_before, lefts, rights, base_done, left_done, right_done = refs
    places, copies = [], []
    for number, (place, index) in enumerate(locate(source, steps)):
        block = arrays[steps[number][0]].at[index]
        pair = (
            pltpu.make_async_copy(late_left.at[number], lefts.at[number], left_done.at[number]),
            pltpu.make_async_copy(block, rights.at[number], right_done.at[number]),
        )
        for copy in pair:
            copy.start()
        places.append(place)
        copies.append(pair)
    fetch = pltpu.make_async_copy(base, sum_before, base_done)
    fetch.start()
    for first in range(0, len(steps), group):
        numbers = range(first, min(first + group, len(steps)))
        for number in numbers:
            for copy in copies[number]:
                copy.wait()
        for tile in range(COLS // TILE):
            cols, real, imag = sum_tile(
                weights,
                tile,
                [places[n] for n in numbers],
                [lefts.at[n] for n in numbers],
                [rights.at[n] for n in numbers],
            )
            if first == 0 and tile == 0:
                fetch.wait()
            before = sum_before if first == 0 else out
            out[0, 0, :, cols] = before[0, 0, :, cols] + real
            out[0, 1, :, cols] = before[0, 1, :, cols] + imag


def cost(count, scale):
    return pl.CostEstimate(
        flops=count * 8 * scale * ROWS * ROWS * COLS,
        bytes_accessed=count * 3 * (1 << 18) + (2 << 20),
        transcendentals=0,
    )


SMEM = pl.BlockSpec(memory_space=pltpu.SMEM)
VMEM = pl.BlockSpec(memory_space=pltpu.VMEM)
HBM = pl.BlockSpec(memory_space=pltpu.HBM)
SUM = jax.ShapeDtypeStruct((1, 2, ROWS, COLS), jnp.float32)


def add_early(weights, source, left, arrays, steps, late):
    count = len(steps)
    return pl.pallas_call(
        functools.partial(sum_early, steps, late, 6),
        out_shape=(SUM, jax.ShapeDtypeStruct((len(late), 2, ROWS, ROWS), jnp.bfloat16)),
        in_specs=[SMEM, SMEM, HBM] + [HBM] * len(arrays),
        out_specs=(VMEM, VMEM),
        scratch_shapes=[
            pltpu.VMEM((count, 2, ROWS, ROWS), jnp.bfloat16),
            pltpu.VMEM((count, 2, ROWS, COLS), jnp.bfloat16),
            pltpu.SemaphoreType.DMA((count,)),
            pltpu.SemaphoreType.DMA((count,)),
            pltpu.SemaphoreType.DMA((len(late),)),
        ],
        compiler_params=pltpu.CompilerParams(vmem_limit_bytes=63 << 20),
        cost_estimate=cost(count, 3),
    )(weights, source, left, *arrays)


def add_late(weights, source, base, late_left, arrays, steps):
    count = len(steps)
    return pl.pallas_call(
        functools.partial(sum_late, steps, 5),
        out_shape=SUM,
        in_specs=[SMEM, SMEM, HBM, HBM] + [HBM] * len(arrays),
        out_specs=VMEM,
        scratch_shapes=[
            pltpu.VMEM((1, 2, ROWS, COLS), jnp.float32),
            pltpu.VMEM((count, 2, ROWS, ROWS), jnp.bfloat16),
            pltpu.VMEM((count, 2, ROWS, COLS), jnp.bfloat16),
            pltpu.SemaphoreType.DMA,
            pltpu.SemaphoreType.DMA((count,)),
            pltpu.SemaphoreType.DMA((count,)),
        ],
        compiler_params=pltpu.CompilerParams(vmem_limit_bytes=60 << 20),
        cost_estimate=cost(count, 3),
    )(weights, source, base, late_left, *arrays)


def shards(recorded, aperture):
    weights = tile_weights(aperture).reshape(8, NB)
    source = lax.axis_index("src")
    x = source % SIDE
    y = source // SIDE
    left = lax.all_gather(recorded, "rcv", axis=3, tiled=True)
    above, below = shift(recorded, 1, 0), shift(recorded, -1, 0)
    before, after = shift(recorded, 0, 1), shift(recorded, 0, -1)
    opposite = shift(recorded, 0, 2)
    across = [shift(above[:, :1], 1, 0), shift(below[:, 1:], -1, 0)]
    *across, before, after, opposite = lax.optimization_barrier((*across, before, after, opposite))
    pair = jnp.concatenate([above, below], axis=0)
    pair_left, pair_right = shift(pair, 0, 1), shift(pair, 0, -1)
    far = jnp.concatenate(across, axis=1)
    across_line = along(far, X_LINES)
    opposite_above, opposite_below = shift(opposite, 1, 0), shift(opposite, -1, 0)

    early = [recorded, above, below, before, after, opposite, pair_left, pair_right, far]
    steps = [(0, 0, 0, 0), (1, 0, 3, 0), (2, 0, 1, 0), (3, 0, 0, 3), (4, 0, 0, 1), (5, 0, 0, 2)]
    steps += [(6, 0, 3, 3), (6, 1, 1, 3), (7, 0, 3, 1), (7, 1, 1, 1)]
    steps += [(8, 0, 2, 0)]
    late = [opposite_above, opposite_below, across_line]
    late_steps = [(0, 0, 3, 2), (1, 0, 1, 2)] + [(2, "x", 2, i) for i in range(1, SIDE)]
    source = source.reshape(1)
    total, late_left = add_early(weights, source, left, early, steps, late_steps)
    return add_late(weights, source, total, late_left, late, late_steps)


def solution(mesh):
    in_specs = (P("grp", None, "src", "rcv"), P(("grp", "src"), "rcv", None))
    out_specs = P("grp", None, "src", "rcv")
    return jax.shard_map(shards, mesh=mesh, in_specs=in_specs, out_specs=out_specs, check_vma=False)
```

time: 117 us -> 111 us (0.949)
  the two profiles are of different devices: /device:TPU:384 before, /device:TPU:450 now
where the time goes in v3:
time: 111 us
  starting transfers between devices  46.9 us (42%)
  waiting for transfers between devices  32.9 us (30%)
  Pallas kernels  14.4 us (13%)
  between operations  13.6 us (12%)
  local copies, waits for them, and re-layouts  2.05 us (2%)
    ppermute x11, starting transfers between devices, shift(): return lax.ppermute(block, 'src', pairs)  41.7 us
    ppermute x11, waiting for transfers between devices, shift(): return lax.ppermute(block, 'src', pairs)  32.2 us
    pallas_call x1, Pallas kernels, add_early(): pl.pallas_call(functools.partial(sum_early, steps, late, 6), out_shape=(S...  8.15 us
    pallas_call x1, Pallas kernels, add_late(): pl.pallas_call(functools.partial(sum_late, steps, 5), out_shape=SUM, in_s...  6.21 us
    all_to_all x1, starting transfers between devices, along(): lax.all_to_all(copies, 'src', 0, 0, tiled=True, axis_index_groups=lines)  5.18 us
  transfers between devices with their start and end apart: 13, of which 7 were waited for; matrix products, arithmetic and copies ran while one was open for 2% of the time, Pallas kernels for 7%

profile of v3, /device:TPU:450, one launch (start us, length us, event | category | flops | bytes accessed | tf_op | source)
XLA Modules:
  0.0 110.5 jit_solution(2664560368081282685)
XLA Ops:
  6.5 0.7 all-gather.2.cloned.1.call-update
  7.3 4.5 %collective-permute-start = (bf16[1,2,256,512]{3,2,1,0:T(8,128)(2,1)}, bf16[1,2,256,512]{3,2,1,0:T(8,128)(2,1)S(1)}, u32[]{:S(2)}, u32[]{:S(2)}) collective-permute-start(bf16[1,2,256,512]{3,2,1,0:T(8,128)(2,1)} %refs_0_.1), channel_id=1, source_target_pairs={{0,32},{8,40},{16,48},{24,56},{32,64},{40,72},{48,80},{56,88},{64,... | collective-permute-start | bytes 1572872 | tf_op jit(solution)/shard_map/ppermute | solution.py:37
  11.8 3.6 %collective-permute-start.1 = (bf16[1,2,256,512]{3,2,1,0:T(8,128)(2,1)}, bf16[1,2,256,512]{3,2,1,0:T(8,128)(2,1)S(1)}, u32[]{:S(2)}, u32[]{:S(2)}) collective-permute-start(bf16[1,2,256,512]{3,2,1,0:T(8,128)(2,1)} %refs_0_.1), channel_id=1, source_target_pairs={{0,96},{8,104},{16,112},{24,120},{32,0},{40,8},{48,16},{56,24},{64... | collective-permute-start | bytes 1572872 | tf_op jit(solution)/shard_map/ppermute | solution.py:37
  15.4 3.4 %collective-permute-start.4 = (bf16[1,2,256,512]{3,2,1,0:T(8,128)(2,1)}, bf16[1,2,256,512]{3,2,1,0:T(8,128)(2,1)S(1)}, u32[]{:S(2)}, u32[]{:S(2)}) collective-permute-start(bf16[1,2,256,512]{3,2,1,0:T(8,128)(2,1)} %refs_0_.1), channel_id=1, source_target_pairs={{0,8},{8,16},{16,24},{24,0},{32,40},{40,48},{48,56},{56,32},{64,72... | collective-permute-start | bytes 1572872 | tf_op jit(solution)/shard_map/ppermute | solution.py:37
  18.8 2.4 %collective-permute-start.5 = (bf16[1,2,256,512]{3,2,1,0:T(8,128)(2,1)}, bf16[1,2,256,512]{3,2,1,0:T(8,128)(2,1)S(1)}, u32[]{:S(2)}, u32[]{:S(2)}) collective-permute-start(bf16[1,2,256,512]{3,2,1,0:T(8,128)(2,1)} %refs_0_.1), channel_id=1, source_target_pairs={{0,24},{8,0},{16,8},{24,16},{32,56},{40,32},{48,40},{56,48},{64,88... | collective-permute-start | bytes 1572872 | tf_op jit(solution)/shard_map/ppermute | solution.py:37
  21.2 4.0 %collective-permute-start.6 = (bf16[1,2,256,512]{3,2,1,0:T(8,128)(2,1)}, bf16[1,2,256,512]{3,2,1,0:T(8,128)(2,1)}, u32[]{:S(2)}, u32[]{:S(2)}) collective-permute-start(bf16[1,2,256,512]{3,2,1,0:T(8,128)(2,1)} %refs_0_.1), channel_id=1, source_target_pairs={{0,16},{8,24},{16,0},{24,8},{32,48},{40,56},{48,32},{56,40},{64,80... | collective-permute-start | bytes 1572872 | tf_op jit(solution)/shard_map/ppermute | solution.py:37
  25.3 7.6 %collective-permute-done.refs_1_ = bf16[1,2,256,512]{3,2,1,0:T(8,128)(2,1)S(1)} collective-permute-done((bf16[1,2,256,512]{3,2,1,0:T(8,128)(2,1)}, bf16[1,2,256,512]{3,2,1,0:T(8,128)(2,1)S(1)}, u32[]{:S(2)}, u32[]{:S(2)}) %collective-permute-start) | collective-permute-done | bytes 524320 | tf_op jit(solution)/shard_map/ppermute | solution.py:37
  32.9 7.2 %collective-permute-start.2 = (bf16[1,1,256,512]{3,2,1,0:T(8,128)(2,1)S(1)}, bf16[1,1,256,512]{3,2,1,0:T(8,128)(2,1)S(1)}, u32[]{:S(2)}, u32[]{:S(2)}) collective-permute-start(bf16[1,1,256,512]{3,2,1,0:T(8,128)(2,1)S(1)} %slice.20), channel_id=1, source_target_pairs={{0,32},{8,40},{16,48},{24,56},{32,64},{40,72},{48,80},{56,88},{64,... | collective-permute-start | bytes 786440 | tf_op jit(solution)/shard_map/ppermute | solution.py:37
  40.1 0.4 collective-permute-done.1.refs_2_
  40.6 3.9 %collective-permute-start.3 = (bf16[1,1,256,512]{3,2,1,0:T(8,128)(2,1)S(1)}, bf16[1,1,256,512]{3,2,1,0:T(8,128)(2,1)S(1)}, u32[]{:S(2)}, u32[]{:S(2)}) collective-permute-start(bf16[1,1,256,512]{3,2,1,0:T(8,128)(2,1)S(1)} %slice.21), channel_id=1, source_target_pairs={{0,96},{8,104},{16,112},{24,120},{32,0},{40,8},{48,16},{56,24},{64... | collective-permute-start | bytes 786440 | tf_op jit(solution)/shard_map/ppermute | solution.py:37
  44.6 0.0 collective-permute-done.4.refs_3_
  44.6 3.4 %collective-permute-start.7 = (bf16[2,2,256,512]{3,2,1,0:T(8,128)(2,1)S(1)}, bf16[2,2,256,512]{3,2,1,0:T(8,128)(2,1)}, u32[]{:S(2)}, u32[]{:S(2)}) collective-permute-start(bf16[2,2,256,512]{3,2,1,0:T(8,128)(2,1)S(1)} %constant_dynamic-update-slice_fusion), channel_id=1, source_target_pairs={{0,8},{8,16},{16,24},{24,0},{32,40},{40,48},{48,56},{56,32},{64,72... | collective-permute-start | bytes 3145736 | tf_op jit(solution)/shard_map/ppermute | solution.py:37
  48.0 0.0 collective-permute-done.5.refs_4_
  48.0 2.4 %collective-permute-start.8 = (bf16[2,2,256,512]{3,2,1,0:T(8,128)(2,1)S(1)}, bf16[2,2,256,512]{3,2,1,0:T(8,128)(2,1)}, u32[]{:S(2)}, u32[]{:S(2)}) collective-permute-start(bf16[2,2,256,512]{3,2,1,0:T(8,128)(2,1)S(1)} %constant_dynamic-update-slice_fusion), channel_id=1, source_target_pairs={{0,24},{8,0},{16,8},{24,16},{32,56},{40,32},{48,40},{56,48},{64,88... | collective-permute-start | bytes 3145736 | tf_op jit(solution)/shard_map/ppermute | solution.py:37
  50.5 0.0 collective-permute-done.6.refs_5_
  50.5 0.0 collective-permute-done.2
  50.5 7.0 %collective-permute-done.3 = bf16[1,1,256,512]{3,2,1,0:T(8,128)(2,1)S(1)} collective-permute-done((bf16[1,1,256,512]{3,2,1,0:T(8,128)(2,1)S(1)}, bf16[1,1,256,512]{3,2,1,0:T(8,128)(2,1)S(1)}, u32[]{:S(2)}, u32[]{:S(2)}) %collective-permute-start.3) | collective-permute-done | bytes 262176 | tf_op jit(solution)/shard_map/ppermute | solution.py:37
  57.6 1.6 %broadcast_in_dim.14 = bf16[4,2,256,512]{3,2,1,0:T(8,128)(2,1)} broadcast(bf16[2,256,512]{2,1,0:T(8,128)(2,1)S(1)} %bitcast.10), dimensions={1,2,3} | broadcast | bytes 2621440 | tf_op jit(solution)/shard_map/broadcast_in_dim | solution.py:41
  59.1 5.2 %all-to-all-start = ((bf16[4,2,256,512]{3,2,1,0:T(8,128)(2,1)}), bf16[4,2,256,512]{3,2,1,0:T(8,128)(2,1)}, u32[]{:S(2)}, u32[]{:S(2)}) async-start(bf16[4,2,256,512]{3,2,1,0:T(8,128)(2,1)} %broadcast_in_dim.14), calls=%async_computation | async-start | bytes 4194304 | tf_op jit(solution)/shard_map/all_to_all | solution.py:42
  64.3 0.1 div.11
  64.4 0.1 lt.11
  64.5 0.1 sub.31
  64.6 0.1 sub.35
  64.6 0.7 fusion.4.weights
  65.3 4.2 %collective-permute-start.10 = (bf16[1,2,256,512]{3,2,1,0:T(8,128)(2,1)}, bf16[1,2,256,512]{3,2,1,0:T(8,128)(2,1)S(1)}, u32[]{:S(2)}, u32[]{:S(2)}) collective-permute-start(bf16[1,2,256,512]{3,2,1,0:T(8,128)(2,1)} %collective-permute-done.6.refs_5_), channel_id=1, source_target_pairs={{0,96},{8,104},{16,112},{24,120},{32,0},{40,8},{48,16},{56,24},{64... | collective-permute-start | bytes 1572872 | tf_op jit(solution)/shard_map/ppermute | solution.py:37
  69.6 2.5 %collective-permute-start.9 = (bf16[1,2,256,512]{3,2,1,0:T(8,128)(2,1)}, bf16[1,2,256,512]{3,2,1,0:T(8,128)(2,1)}, u32[]{:S(2)}, u32[]{:S(2)}) collective-permute-start(bf16[1,2,256,512]{3,2,1,0:T(8,128)(2,1)} %collective-permute-done.6.refs_5_), channel_id=1, source_target_pairs={{0,32},{8,40},{16,48},{24,56},{32,64},{40,72},{48,80},{56,88},{64,... | collective-permute-start | bytes 1572872 | tf_op jit(solution)/shard_map/ppermute | solution.py:37
  72.1 0.6 collective-permute-done.7.refs_6_
  72.7 3.4 %collective-permute-done.8.refs_7_ = bf16[2,2,256,512]{3,2,1,0:T(8,128)(2,1)} collective-permute-done((bf16[2,2,256,512]{3,2,1,0:T(8,128)(2,1)S(1)}, bf16[2,2,256,512]{3,2,1,0:T(8,128)(2,1)}, u32[]{:S(2)}, u32[]{:S(2)}) %collective-permute-start.8) | collective-permute-done | bytes 1048608 | tf_op jit(solution)/shard_map/ppermute | solution.py:37
  76.1 8.1 %shard_map.28 = (f32[1,2,256,512]{3,2,1,0:T(8,128)}, bf16[5,2,256,256]{3,2,1,0:T(8,128)(2,1)}) custom-call(f32[8,32]{1,0:T(8,128)} %fusion.4.weights, s32[1]{0:T(128)} %bitcast.source, bf16[1,2,256,4096]{3,2,1,0:T(8,128)(2,1)} %all-gather.2.cloned.1.call-done.left, bf16[1,2,256,512]{3,2,1,0:T(8,128)(2,1)} %refs_0_.1, bf16[1,2,256,512]{3,2,1,0:T(8,128)(2,1)} %copy-done.1, ...), custom_call_target="tpu_custom_call" | custom-call | flops 8858370048 | bytes 10747904 | tf_op jit(solution)/shard_map/pallas_call | solution.py:172
  84.3 2.5 %collective-permute-done.10.refs_1_ = bf16[1,2,256,512]{3,2,1,0:T(8,128)(2,1)S(1)} collective-permute-done((bf16[1,2,256,512]{3,2,1,0:T(8,128)(2,1)}, bf16[1,2,256,512]{3,2,1,0:T(8,128)(2,1)S(1)}, u32[]{:S(2)}, u32[]{:S(2)}) %collective-permute-start.10) | collective-permute-done | bytes 524320 | tf_op jit(solution)/shard_map/ppermute | solution.py:37
  86.7 10.7 %collective-permute-done.9.refs_0_ = bf16[1,2,256,512]{3,2,1,0:T(8,128)(2,1)} collective-permute-done((bf16[1,2,256,512]{3,2,1,0:T(8,128)(2,1)}, bf16[1,2,256,512]{3,2,1,0:T(8,128)(2,1)}, u32[]{:S(2)}, u32[]{:S(2)}) %collective-permute-start.9) | collective-permute-done | bytes 524320 | tf_op jit(solution)/shard_map/ppermute | solution.py:37
  97.5 6.2 %shard_map.29 = f32[1,2,256,512]{3,2,1,0:T(8,128)} custom-call(f32[8,32]{1,0:T(8,128)} %fusion.4.weights, s32[1]{0:T(128)} %bitcast.source, f32[1,2,256,512]{3,2,1,0:T(8,128)} %get-tuple-element.17.base, bf16[5,2,256,256]{3,2,1,0:T(8,128)(2,1)} %get-tuple-element.18.late_left, bf16[1,2,256,512]{3,2,1,0:T(8,128)(2,1)} %collective-permute-done.9.refs_0_, ...), custom_call_target="tpu_custom_call" | custom-call | flops 4026531840 | bytes 6029312 | tf_op jit(solution)/shard_map/pallas_call | solution.py:191
  (24 shorter events, 0.2 us)
Async XLA Ops:
  6.5 69.6 %all-gather.2.cloned.1.call-start = ((), (), s32[]{:S(2)}) async-start(), calls=%async_computation.1 | async-start | bytes 4718592 | tf_op jit(solution)/shard_map/all_gather | solution.py:214
  7.3 25.6 %collective-permute-start = (bf16[1,2,256,512]{3,2,1,0:T(8,128)(2,1)}, bf16[1,2,256,512]{3,2,1,0:T(8,128)(2,1)S(1)}, u32[]{:S(2)}, u32[]{:S(2)}) collective-permute-start(bf16[1,2,256,512]{3,2,1,0:T(8,128)(2,1)} %refs_0_.1), channel_id=1, source_target_pairs={{0,32},{8,40},{16,48},{24,56},{32,64},{40,72},{48,80},{56,88},{64,... | collective-permute-start | bytes 1572872 | tf_op jit(solution)/shard_map/ppermute | solution.py:37
  11.8 28.8 %collective-permute-start.1 = (bf16[1,2,256,512]{3,2,1,0:T(8,128)(2,1)}, bf16[1,2,256,512]{3,2,1,0:T(8,128)(2,1)S(1)}, u32[]{:S(2)}, u32[]{:S(2)}) collective-permute-start(bf16[1,2,256,512]{3,2,1,0:T(8,128)(2,1)} %refs_0_.1), channel_id=1, source_target_pairs={{0,96},{8,104},{16,112},{24,120},{32,0},{40,8},{48,16},{56,24},{64... | collective-permute-start | bytes 1572872 | tf_op jit(solution)/shard_map/ppermute | solution.py:37
  15.4 29.2 %collective-permute-start.4 = (bf16[1,2,256,512]{3,2,1,0:T(8,128)(2,1)}, bf16[1,2,256,512]{3,2,1,0:T(8,128)(2,1)S(1)}, u32[]{:S(2)}, u32[]{:S(2)}) collective-permute-start(bf16[1,2,256,512]{3,2,1,0:T(8,128)(2,1)} %refs_0_.1), channel_id=1, source_target_pairs={{0,8},{8,16},{16,24},{24,0},{32,40},{40,48},{48,56},{56,32},{64,72... | collective-permute-start | bytes 1572872 | tf_op jit(solution)/shard_map/ppermute | solution.py:37
  18.8 29.2 %collective-permute-start.5 = (bf16[1,2,256,512]{3,2,1,0:T(8,128)(2,1)}, bf16[1,2,256,512]{3,2,1,0:T(8,128)(2,1)S(1)}, u32[]{:S(2)}, u32[]{:S(2)}) collective-permute-start(bf16[1,2,256,512]{3,2,1,0:T(8,128)(2,1)} %refs_0_.1), channel_id=1, source_target_pairs={{0,24},{8,0},{16,8},{24,16},{32,56},{40,32},{48,40},{56,48},{64,88... | collective-permute-start | bytes 1572872 | tf_op jit(solution)/shard_map/ppermute | solution.py:37
  21.2 29.3 %collective-permute-start.6 = (bf16[1,2,256,512]{3,2,1,0:T(8,128)(2,1)}, bf16[1,2,256,512]{3,2,1,0:T(8,128)(2,1)}, u32[]{:S(2)}, u32[]{:S(2)}) collective-permute-start(bf16[1,2,256,512]{3,2,1,0:T(8,128)(2,1)} %refs_0_.1), channel_id=1, source_target_pairs={{0,16},{8,24},{16,0},{24,8},{32,48},{40,56},{48,32},{56,40},{64,80... | collective-permute-start | bytes 1572872 | tf_op jit(solution)/shard_map/ppermute | solution.py:37
  32.8 24.7 %copy-start.1 = (bf16[1,2,256,512]{3,2,1,0:T(8,128)(2,1)}, bf16[1,2,256,512]{3,2,1,0:T(8,128)(2,1)S(1)}, u32[]{:S(2)}) copy-start(bf16[1,2,256,512]{3,2,1,0:T(8,128)(2,1)S(1)} %collective-permute-done.refs_1_) | copy-start | bytes 1572868
  32.9 17.6 %collective-permute-start.2 = (bf16[1,1,256,512]{3,2,1,0:T(8,128)(2,1)S(1)}, bf16[1,1,256,512]{3,2,1,0:T(8,128)(2,1)S(1)}, u32[]{:S(2)}, u32[]{:S(2)}) collective-permute-start(bf16[1,1,256,512]{3,2,1,0:T(8,128)(2,1)S(1)} %slice.20), channel_id=1, source_target_pairs={{0,32},{8,40},{16,48},{24,56},{32,64},{40,72},{48,80},{56,88},{64,... | collective-permute-start | bytes 786440 | tf_op jit(solution)/shard_map/ppermute | solution.py:37
  40.6 17.0 %copy-start.2 = (bf16[1,2,256,512]{3,2,1,0:T(8,128)(2,1)}, bf16[1,2,256,512]{3,2,1,0:T(8,128)(2,1)S(1)}, u32[]{:S(2)}) copy-start(bf16[1,2,256,512]{3,2,1,0:T(8,128)(2,1)S(1)} %collective-permute-done.1.refs_2_) | copy-start | bytes 1572868
  40.6 16.9 %collective-permute-start.3 = (bf16[1,1,256,512]{3,2,1,0:T(8,128)(2,1)S(1)}, bf16[1,1,256,512]{3,2,1,0:T(8,128)(2,1)S(1)}, u32[]{:S(2)}, u32[]{:S(2)}) collective-permute-start(bf16[1,1,256,512]{3,2,1,0:T(8,128)(2,1)S(1)} %slice.21), channel_id=1, source_target_pairs={{0,96},{8,104},{16,112},{24,120},{32,0},{40,8},{48,16},{56,24},{64... | collective-permute-start | bytes 786440 | tf_op jit(solution)/shard_map/ppermute | solution.py:37
  44.6 12.9 %copy-start.4 = (bf16[1,2,256,512]{3,2,1,0:T(8,128)(2,1)}, bf16[1,2,256,512]{3,2,1,0:T(8,128)(2,1)S(1)}, u32[]{:S(2)}) copy-start(bf16[1,2,256,512]{3,2,1,0:T(8,128)(2,1)S(1)} %collective-permute-done.4.refs_3_) | copy-start | bytes 1572868
  44.6 28.1 %collective-permute-start.7 = (bf16[2,2,256,512]{3,2,1,0:T(8,128)(2,1)S(1)}, bf16[2,2,256,512]{3,2,1,0:T(8,128)(2,1)}, u32[]{:S(2)}, u32[]{:S(2)}) collective-permute-start(bf16[2,2,256,512]{3,2,1,0:T(8,128)(2,1)S(1)} %constant_dynamic-update-slice_fusion), channel_id=1, source_target_pairs={{0,8},{8,16},{16,24},{24,0},{32,40},{40,48},{48,56},{56,32},{64,72... | collective-permute-start | bytes 3145736 | tf_op jit(solution)/shard_map/ppermute | solution.py:37
  48.0 9.5 %copy-start.5 = (bf16[1,2,256,512]{3,2,1,0:T(8,128)(2,1)}, bf16[1,2,256,512]{3,2,1,0:T(8,128)(2,1)S(1)}, u32[]{:S(2)}) copy-start(bf16[1,2,256,512]{3,2,1,0:T(8,128)(2,1)S(1)} %collective-permute-done.5.refs_4_) | copy-start | bytes 1572868
  48.0 28.1 %collective-permute-start.8 = (bf16[2,2,256,512]{3,2,1,0:T(8,128)(2,1)S(1)}, bf16[2,2,256,512]{3,2,1,0:T(8,128)(2,1)}, u32[]{:S(2)}, u32[]{:S(2)}) collective-permute-start(bf16[2,2,256,512]{3,2,1,0:T(8,128)(2,1)S(1)} %constant_dynamic-update-slice_fusion), channel_id=1, source_target_pairs={{0,24},{8,0},{16,8},{24,16},{32,56},{40,32},{48,40},{56,48},{64,88... | collective-permute-start | bytes 3145736 | tf_op jit(solution)/shard_map/ppermute | solution.py:37
  57.6 1.6 %copy-start = (bf16[1,2,256,512]{3,2,1,0:T(8,128)(2,1)}, bf16[1,2,256,512]{3,2,1,0:T(8,128)(2,1)S(1)}, u32[]{:S(2)}) copy-start(bf16[1,2,256,512]{3,2,1,0:T(8,128)(2,1)S(1)} %constant_dynamic-update-slice_fusion.2.refs_8_) | copy-start | bytes 1572868
  59.1 5.2 %copy-start.3 = (s32[2,4,3]{1,0,2:T(2,128)S(1)}, s32[2,4,3]{1,0,2:T(2,128)}, u32[]{:S(2)}) copy-start(s32[2,4,3]{1,0,2:T(2,128)} %param.3) | copy-start | bytes 292
  59.1 38.3 %all-to-all-start = ((bf16[4,2,256,512]{3,2,1,0:T(8,128)(2,1)}), bf16[4,2,256,512]{3,2,1,0:T(8,128)(2,1)}, u32[]{:S(2)}, u32[]{:S(2)}) async-start(bf16[4,2,256,512]{3,2,1,0:T(8,128)(2,1)} %broadcast_in_dim.14), calls=%async_computation | async-start | bytes 4194304 | tf_op jit(solution)/shard_map/all_to_all | solution.py:42
  65.3 21.4 %collective-permute-start.10 = (bf16[1,2,256,512]{3,2,1,0:T(8,128)(2,1)}, bf16[1,2,256,512]{3,2,1,0:T(8,128)(2,1)S(1)}, u32[]{:S(2)}, u32[]{:S(2)}) collective-permute-start(bf16[1,2,256,512]{3,2,1,0:T(8,128)(2,1)} %collective-permute-done.6.refs_5_), channel_id=1, source_target_pairs={{0,96},{8,104},{16,112},{24,120},{32,0},{40,8},{48,16},{56,24},{64... | collective-permute-start | bytes 1572872 | tf_op jit(solution)/shard_map/ppermute | solution.py:37
  69.6 27.9 %collective-permute-start.9 = (bf16[1,2,256,512]{3,2,1,0:T(8,128)(2,1)}, bf16[1,2,256,512]{3,2,1,0:T(8,128)(2,1)}, u32[]{:S(2)}, u32[]{:S(2)}) collective-permute-start(bf16[1,2,256,512]{3,2,1,0:T(8,128)(2,1)} %collective-permute-done.6.refs_5_), channel_id=1, source_target_pairs={{0,32},{8,40},{16,48},{24,56},{32,64},{40,72},{48,80},{56,88},{64,... | collective-permute-start | bytes 1572872 | tf_op jit(solution)/shard_map/ppermute | solution.py:37
  86.7 10.7 %copy-start.6 = (bf16[1,2,256,512]{3,2,1,0:T(8,128)(2,1)}, bf16[1,2,256,512]{3,2,1,0:T(8,128)(2,1)S(1)}, u32[]{:S(2)}) copy-start(bf16[1,2,256,512]{3,2,1,0:T(8,128)(2,1)S(1)} %collective-permute-done.10.refs_1_) | copy-start | bytes 1572868
Sparse Core Ops, SparseCore 0:
  9.4 55.1 all-gather.1

commit v4 on v3

--- a/solution.py
+++ b/solution.py
@@ -119,7 +119,7 @@
 
 
 def sum_late(steps, group, weights, source, base, late_left, *refs):
-    *arrays, out, sum_before, lefts, rights, base_done, left_done, right_done = refs
+    *arrays, out, total, partial, lefts, rights, left_done, right_done, base_done, out_done = refs
     places, copies = [], []
     for number, (place, index) in enumerate(locate(source, steps)):
         block = arrays[steps[number][0]].at[index]
@@ -131,13 +131,15 @@
             copy.start()
         places.append(place)
         copies.append(pair)
-    fetch = pltpu.make_async_copy(base, sum_before, base_done)
+    fetch = pltpu.make_async_copy(base, total, base_done)
     fetch.start()
+    stores = []
     for first in range(0, len(steps), group):
         numbers = range(first, min(first + group, len(steps)))
         for number in numbers:
             for copy in copies[number]:
                 copy.wait()
+        last = first + group >= len(steps)
         for tile in range(COLS // TILE):
             cols, real, imag = sum_tile(
                 weights,
@@ -146,11 +148,24 @@
                 [lefts.at[n] for n in numbers],
                 [rights.at[n] for n in numbers],
             )
-            if first == 0 and tile == 0:
+            if last and first > 0 and tile == 0:
                 fetch.wait()
-            before = sum_before if first == 0 else out
-            out[0, 0, :, cols] = before[0, 0, :, cols] + real
-            out[0, 1, :, cols] = before[0, 1, :, cols] + imag
+            if first > 0:
+                real, imag = real + partial[0, :, cols], imag + partial[1, :, cols]
+            if last:
+                total[0, 0, :, cols] += real
+                total[0, 1, :, cols] += imag
+            else:
+                partial[0, :, cols] = real
+                partial[1, :, cols] = imag
+            if last:
+                store = pltpu.make_async_copy(
+                    total.at[0, :, :, cols], out.at[0, :, :, cols], out_done.at[tile]
+                )
+                store.start()
+                stores.append(store)
+    for store in stores:
+        store.wait()
 
 
 def cost(count, scale):
@@ -189,17 +204,19 @@
 def add_late(weights, source, base, late_left, arrays, steps):
     count = len(steps)
     return pl.pallas_call(
-        functools.partial(sum_late, steps, 5),
+        functools.partial(sum_late, steps, 2),
         out_shape=SUM,
         in_specs=[SMEM, SMEM, HBM, HBM] + [HBM] * len(arrays),
-        out_specs=VMEM,
+        out_specs=HBM,
         scratch_shapes=[
             pltpu.VMEM((1, 2, ROWS, COLS), jnp.float32),
+            pltpu.VMEM((2, ROWS, COLS), jnp.float32),
             pltpu.VMEM((count, 2, ROWS, ROWS), jnp.bfloat16),
             pltpu.VMEM((count, 2, ROWS, COLS), jnp.bfloat16),
+            pltpu.SemaphoreType.DMA((count,)),
+            pltpu.SemaphoreType.DMA((count,)),
             pltpu.SemaphoreType.DMA,
-            pltpu.SemaphoreType.DMA((count,)),
-            pltpu.SemaphoreType.DMA((count,)),
+            pltpu.SemaphoreType.DMA((COLS // TILE,)),
         ],
         compiler_params=pltpu.CompilerParams(vmem_limit_bytes=60 << 20),
         cost_estimate=cost(count, 3),
@@ -216,7 +233,9 @@
     before, after = shift(recorded, 0, 1), shift(recorded, 0, -1)
     opposite = shift(recorded, 0, 2)
     across = [shift(above[:, :1], 1, 0), shift(below[:, 1:], -1, 0)]
-    *across, before, after, opposite = lax.optimization_barrier((*across, before, after, opposite))
+    *across, before, after, opposite, weights = lax.optimization_barrier(
+        (*across, before, after, opposite, weights)
+    )
     pair = jnp.concatenate([above, below], axis=0)
     pair_left, pair_right = shift(pair, 0, 1), shift(pair, 0, -1)
     far = jnp.concatenate(across, axis=1)

time: 111 us -> 110 us (level)
  the two profiles are of different devices: /device:TPU:450 before, /device:TPU:386 now
where the time goes in v4:
time: 110 us; the launch traced here: 109 us
  starting transfers between devices  46.7 us (42%)
  waiting for transfers between devices  32.1 us (29%)
  between operations  13.6 us (12%)
  Pallas kernels  13.4 us (12%)
  local copies, waits for them, and re-layouts  2.05 us (2%)
  other arithmetic  1.39 us (1%)
    ppermute x11, starting transfers between devices, shift(): return lax.ppermute(block, 'src', pairs)  41.7 us
    ppermute x11, waiting for transfers between devices, shift(): return lax.ppermute(block, 'src', pairs)  30.4 us
    pallas_call x1, Pallas kernels, add_early(): pl.pallas_call(functools.partial(sum_early, steps, late, 6), out_shape=(S...  8.15 us
    pallas_call x1, Pallas kernels, add_late(): pl.pallas_call(functools.partial(sum_late, steps, 2), out_shape=SUM, in_s...  5.21 us
    all_to_all x1, starting transfers between devices, along(): lax.all_to_all(copies, 'src', 0, 0, tiled=True, axis_index_groups=lines)  5.05 us
  transfers between devices with their start and end apart: 13, of which 8 were waited for; matrix products, arithmetic and copies ran while one was open for 3% of the time, Pallas kernels for 7%

profile of v4, /device:TPU:386, one launch (start us, length us, event | category | flops | bytes accessed | tf_op | source)
XLA Modules:
  0.0 109.2 jit_solution(14935374734241886908)
XLA Ops:
  6.5 0.7 all-gather.2.cloned.1.call-update
  7.3 4.5 %collective-permute-start = (bf16[1,2,256,512]{3,2,1,0:T(8,128)(2,1)}, bf16[1,2,256,512]{3,2,1,0:T(8,128)(2,1)S(1)}, u32[]{:S(2)}, u32[]{:S(2)}) collective-permute-start(bf16[1,2,256,512]{3,2,1,0:T(8,128)(2,1)} %refs_0_.1), channel_id=1, source_target_pairs={{0,32},{8,40},{16,48},{24,56},{32,64},{40,72},{48,80},{56,88},{64,... | collective-permute-start | bytes 1572872 | tf_op jit(solution)/shard_map/ppermute | solution.py:37
  11.8 3.6 %collective-permute-start.2 = (bf16[1,2,256,512]{3,2,1,0:T(8,128)(2,1)}, bf16[1,2,256,512]{3,2,1,0:T(8,128)(2,1)S(1)}, u32[]{:S(2)}, u32[]{:S(2)}) collective-permute-start(bf16[1,2,256,512]{3,2,1,0:T(8,128)(2,1)} %refs_0_.1), channel_id=1, source_target_pairs={{0,96},{8,104},{16,112},{24,120},{32,0},{40,8},{48,16},{56,24},{64... | collective-permute-start | bytes 1572872 | tf_op jit(solution)/shard_map/ppermute | solution.py:37
  15.4 3.4 %collective-permute-start.4 = (bf16[1,2,256,512]{3,2,1,0:T(8,128)(2,1)}, bf16[1,2,256,512]{3,2,1,0:T(8,128)(2,1)S(1)}, u32[]{:S(2)}, u32[]{:S(2)}) collective-permute-start(bf16[1,2,256,512]{3,2,1,0:T(8,128)(2,1)} %refs_0_.1), channel_id=1, source_target_pairs={{0,8},{8,16},{16,24},{24,0},{32,40},{40,48},{48,56},{56,32},{64,72... | collective-permute-start | bytes 1572872 | tf_op jit(solution)/shard_map/ppermute | solution.py:37
  18.8 2.4 %collective-permute-start.5 = (bf16[1,2,256,512]{3,2,1,0:T(8,128)(2,1)}, bf16[1,2,256,512]{3,2,1,0:T(8,128)(2,1)S(1)}, u32[]{:S(2)}, u32[]{:S(2)}) collective-permute-start(bf16[1,2,256,512]{3,2,1,0:T(8,128)(2,1)} %refs_0_.1), channel_id=1, source_target_pairs={{0,24},{8,0},{16,8},{24,16},{32,56},{40,32},{48,40},{56,48},{64,88... | collective-permute-start | bytes 1572872 | tf_op jit(solution)/shard_map/ppermute | solution.py:37
  21.2 4.0 %collective-permute-start.6 = (bf16[1,2,256,512]{3,2,1,0:T(8,128)(2,1)}, bf16[1,2,256,512]{3,2,1,0:T(8,128)(2,1)}, u32[]{:S(2)}, u32[]{:S(2)}) collective-permute-start(bf16[1,2,256,512]{3,2,1,0:T(8,128)(2,1)} %refs_0_.1), channel_id=1, source_target_pairs={{0,16},{8,24},{16,0},{24,8},{32,48},{40,56},{48,32},{56,40},{64,80... | collective-permute-start | bytes 1572872 | tf_op jit(solution)/shard_map/ppermute | solution.py:37
  25.3 0.7 fusion.8
  26.0 0.1 div.11
  26.1 0.1 lt.11
  26.1 0.1 sub.31
  26.2 0.1 sub.35
  26.3 6.5 %collective-permute-done.refs_1_ = bf16[1,2,256,512]{3,2,1,0:T(8,128)(2,1)S(1)} collective-permute-done((bf16[1,2,256,512]{3,2,1,0:T(8,128)(2,1)}, bf16[1,2,256,512]{3,2,1,0:T(8,128)(2,1)S(1)}, u32[]{:S(2)}, u32[]{:S(2)}) %collective-permute-start) | collective-permute-done | bytes 524320 | tf_op jit(solution)/shard_map/ppermute | solution.py:37
  32.9 7.2 %collective-permute-start.1 = (bf16[1,1,256,512]{3,2,1,0:T(8,128)(2,1)S(1)}, bf16[1,1,256,512]{3,2,1,0:T(8,128)(2,1)S(1)}, u32[]{:S(2)}, u32[]{:S(2)}) collective-permute-start(bf16[1,1,256,512]{3,2,1,0:T(8,128)(2,1)S(1)} %slice.20), channel_id=1, source_target_pairs={{0,32},{8,40},{16,48},{24,56},{32,64},{40,72},{48,80},{56,88},{64,... | collective-permute-start | bytes 786440 | tf_op jit(solution)/shard_map/ppermute | solution.py:37
  40.1 0.4 collective-permute-done.2.refs_2_
  40.6 3.9 %collective-permute-start.3 = (bf16[1,1,256,512]{3,2,1,0:T(8,128)(2,1)S(1)}, bf16[1,1,256,512]{3,2,1,0:T(8,128)(2,1)S(1)}, u32[]{:S(2)}, u32[]{:S(2)}) collective-permute-start(bf16[1,1,256,512]{3,2,1,0:T(8,128)(2,1)S(1)} %slice.21), channel_id=1, source_target_pairs={{0,96},{8,104},{16,112},{24,120},{32,0},{40,8},{48,16},{56,24},{64... | collective-permute-start | bytes 786440 | tf_op jit(solution)/shard_map/ppermute | solution.py:37
  44.6 3.4 %collective-permute-start.7 = (bf16[2,2,256,512]{3,2,1,0:T(8,128)(2,1)S(1)}, bf16[2,2,256,512]{3,2,1,0:T(8,128)(2,1)}, u32[]{:S(2)}, u32[]{:S(2)}) collective-permute-start(bf16[2,2,256,512]{3,2,1,0:T(8,128)(2,1)S(1)} %constant_dynamic-update-slice_fusion), channel_id=1, source_target_pairs={{0,8},{8,16},{16,24},{24,0},{32,40},{40,48},{48,56},{56,32},{64,72... | collective-permute-start | bytes 3145736 | tf_op jit(solution)/shard_map/ppermute | solution.py:37
  48.0 0.0 collective-permute-done.5.refs_4_
  48.0 2.4 %collective-permute-start.8 = (bf16[2,2,256,512]{3,2,1,0:T(8,128)(2,1)S(1)}, bf16[2,2,256,512]{3,2,1,0:T(8,128)(2,1)}, u32[]{:S(2)}, u32[]{:S(2)}) collective-permute-start(bf16[2,2,256,512]{3,2,1,0:T(8,128)(2,1)S(1)} %constant_dynamic-update-slice_fusion), channel_id=1, source_target_pairs={{0,24},{8,0},{16,8},{24,16},{32,56},{40,32},{48,40},{56,48},{64,88... | collective-permute-start | bytes 3145736 | tf_op jit(solution)/shard_map/ppermute | solution.py:37
  50.5 0.7 fusion.4.weights
  51.2 0.0 collective-permute-done.6.refs_5_
  51.2 6.3 %collective-permute-done.3 = bf16[1,1,256,512]{3,2,1,0:T(8,128)(2,1)S(1)} collective-permute-done((bf16[1,1,256,512]{3,2,1,0:T(8,128)(2,1)S(1)}, bf16[1,1,256,512]{3,2,1,0:T(8,128)(2,1)S(1)}, u32[]{:S(2)}, u32[]{:S(2)}) %collective-permute-start.3) | collective-permute-done | bytes 262176 | tf_op jit(solution)/shard_map/ppermute | solution.py:37
  57.5 1.6 %broadcast_in_dim.14 = bf16[4,2,256,512]{3,2,1,0:T(8,128)(2,1)} broadcast(bf16[2,256,512]{2,1,0:T(8,128)(2,1)S(1)} %bitcast.10), dimensions={1,2,3} | broadcast | bytes 2621440 | tf_op jit(solution)/shard_map/broadcast_in_dim | solution.py:41
  59.1 5.1 %all-to-all-start = ((bf16[4,2,256,512]{3,2,1,0:T(8,128)(2,1)}), bf16[4,2,256,512]{3,2,1,0:T(8,128)(2,1)}, u32[]{:S(2)}, u32[]{:S(2)}) async-start(bf16[4,2,256,512]{3,2,1,0:T(8,128)(2,1)} %broadcast_in_dim.14), calls=%async_computation | async-start | bytes 4194304 | tf_op jit(solution)/shard_map/all_to_all | solution.py:42
  64.2 4.2 %collective-permute-start.10 = (bf16[1,2,256,512]{3,2,1,0:T(8,128)(2,1)}, bf16[1,2,256,512]{3,2,1,0:T(8,128)(2,1)S(1)}, u32[]{:S(2)}, u32[]{:S(2)}) collective-permute-start(bf16[1,2,256,512]{3,2,1,0:T(8,128)(2,1)} %collective-permute-done.6.refs_5_), channel_id=1, source_target_pairs={{0,96},{8,104},{16,112},{24,120},{32,0},{40,8},{48,16},{56,24},{64... | collective-permute-start | bytes 1572872 | tf_op jit(solution)/shard_map/ppermute | solution.py:37
  68.4 2.5 %collective-permute-start.9 = (bf16[1,2,256,512]{3,2,1,0:T(8,128)(2,1)}, bf16[1,2,256,512]{3,2,1,0:T(8,128)(2,1)}, u32[]{:S(2)}, u32[]{:S(2)}) collective-permute-start(bf16[1,2,256,512]{3,2,1,0:T(8,128)(2,1)} %collective-permute-done.6.refs_5_), channel_id=1, source_target_pairs={{0,32},{8,40},{16,48},{24,56},{32,64},{40,72},{48,80},{56,88},{64,... | collective-permute-start | bytes 1572872 | tf_op jit(solution)/shard_map/ppermute | solution.py:37
  70.9 1.8 %collective-permute-done.7.refs_6_ = bf16[2,2,256,512]{3,2,1,0:T(8,128)(2,1)} collective-permute-done((bf16[2,2,256,512]{3,2,1,0:T(8,128)(2,1)S(1)}, bf16[2,2,256,512]{3,2,1,0:T(8,128)(2,1)}, u32[]{:S(2)}, u32[]{:S(2)}) %collective-permute-start.7) | collective-permute-done | bytes 1048608 | tf_op jit(solution)/shard_map/ppermute | solution.py:37
  72.7 3.4 %collective-permute-done.8.refs_7_ = bf16[2,2,256,512]{3,2,1,0:T(8,128)(2,1)} collective-permute-done((bf16[2,2,256,512]{3,2,1,0:T(8,128)(2,1)S(1)}, bf16[2,2,256,512]{3,2,1,0:T(8,128)(2,1)}, u32[]{:S(2)}, u32[]{:S(2)}) %collective-permute-start.8) | collective-permute-done | bytes 1048608 | tf_op jit(solution)/shard_map/ppermute | solution.py:37
  76.1 8.1 %shard_map.28 = (f32[1,2,256,512]{3,2,1,0:T(8,128)}, bf16[5,2,256,256]{3,2,1,0:T(8,128)(2,1)}) custom-call(f32[8,32]{1,0:T(8,128)} %fusion.4.weights, s32[1]{0:T(128)} %bitcast.source, bf16[1,2,256,4096]{3,2,1,0:T(8,128)(2,1)} %all-gather.2.cloned.1.call-done.left, bf16[1,2,256,512]{3,2,1,0:T(8,128)(2,1)} %refs_0_.1, bf16[1,2,256,512]{3,2,1,0:T(8,128)(2,1)} %copy-done.1, ...), custom_call_target="tpu_custom_call" | custom-call | flops 8858370048 | bytes 10747904 | tf_op jit(solution)/shard_map/pallas_call | solution.py:187
  84.3 1.3 %collective-permute-done.10.refs_1_ = bf16[1,2,256,512]{3,2,1,0:T(8,128)(2,1)S(1)} collective-permute-done((bf16[1,2,256,512]{3,2,1,0:T(8,128)(2,1)}, bf16[1,2,256,512]{3,2,1,0:T(8,128)(2,1)S(1)}, u32[]{:S(2)}, u32[]{:S(2)}) %collective-permute-start.10) | collective-permute-done | bytes 524320 | tf_op jit(solution)/shard_map/ppermute | solution.py:37
  85.6 10.6 %collective-permute-done.9.refs_0_ = bf16[1,2,256,512]{3,2,1,0:T(8,128)(2,1)} collective-permute-done((bf16[1,2,256,512]{3,2,1,0:T(8,128)(2,1)}, bf16[1,2,256,512]{3,2,1,0:T(8,128)(2,1)}, u32[]{:S(2)}, u32[]{:S(2)}) %collective-permute-start.9) | collective-permute-done | bytes 524320 | tf_op jit(solution)/shard_map/ppermute | solution.py:37
  96.2 0.9 all-to-all-done.refs_2_
  97.1 5.2 %shard_map.29 = f32[1,2,256,512]{3,2,1,0:T(8,128)} custom-call(f32[8,32]{1,0:T(8,128)} %fusion.4.weights, s32[1]{0:T(128)} %bitcast.source, f32[1,2,256,512]{3,2,1,0:T(8,128)} %get-tuple-element.19.base, bf16[5,2,256,256]{3,2,1,0:T(8,128)(2,1)} %get-tuple-element.20.late_left, bf16[1,2,256,512]{3,2,1,0:T(8,128)(2,1)} %collective-permute-done.9.refs_0_, ...), custom_call_target="tpu_custom_call" | custom-call | flops 4026531840 | bytes 6029312 | tf_op jit(solution)/shard_map/pallas_call | solution.py:206
  (22 shorter events, 0.2 us)
Async XLA Ops:
  6.5 69.6 %all-gather.2.cloned.1.call-start = ((), (), s32[]{:S(2)}) async-start(), calls=%async_computation.1 | async-start | bytes 4718592 | tf_op jit(solution)/shard_map/all_gather | solution.py:231
  7.3 25.6 %collective-permute-start = (bf16[1,2,256,512]{3,2,1,0:T(8,128)(2,1)}, bf16[1,2,256,512]{3,2,1,0:T(8,128)(2,1)S(1)}, u32[]{:S(2)}, u32[]{:S(2)}) collective-permute-start(bf16[1,2,256,512]{3,2,1,0:T(8,128)(2,1)} %refs_0_.1), channel_id=1, source_target_pairs={{0,32},{8,40},{16,48},{24,56},{32,64},{40,72},{48,80},{56,88},{64,... | collective-permute-start | bytes 1572872 | tf_op jit(solution)/shard_map/ppermute | solution.py:37
  11.8 28.8 %collective-permute-start.2 = (bf16[1,2,256,512]{3,2,1,0:T(8,128)(2,1)}, bf16[1,2,256,512]{3,2,1,0:T(8,128)(2,1)S(1)}, u32[]{:S(2)}, u32[]{:S(2)}) collective-permute-start(bf16[1,2,256,512]{3,2,1,0:T(8,128)(2,1)} %refs_0_.1), channel_id=1, source_target_pairs={{0,96},{8,104},{16,112},{24,120},{32,0},{40,8},{48,16},{56,24},{64... | collective-permute-start | bytes 1572872 | tf_op jit(solution)/shard_map/ppermute | solution.py:37
  15.4 29.2 %collective-permute-start.4 = (bf16[1,2,256,512]{3,2,1,0:T(8,128)(2,1)}, bf16[1,2,256,512]{3,2,1,0:T(8,128)(2,1)S(1)}, u32[]{:S(2)}, u32[]{:S(2)}) collective-permute-start(bf16[1,2,256,512]{3,2,1,0:T(8,128)(2,1)} %refs_0_.1), channel_id=1, source_target_pairs={{0,8},{8,16},{16,24},{24,0},{32,40},{40,48},{48,56},{56,32},{64,72... | collective-permute-start | bytes 1572872 | tf_op jit(solution)/shard_map/ppermute | solution.py:37
  18.8 29.2 %collective-permute-start.5 = (bf16[1,2,256,512]{3,2,1,0:T(8,128)(2,1)}, bf16[1,2,256,512]{3,2,1,0:T(8,128)(2,1)S(1)}, u32[]{:S(2)}, u32[]{:S(2)}) collective-permute-start(bf16[1,2,256,512]{3,2,1,0:T(8,128)(2,1)} %refs_0_.1), channel_id=1, source_target_pairs={{0,24},{8,0},{16,8},{24,16},{32,56},{40,32},{48,40},{56,48},{64,88... | collective-permute-start | bytes 1572872 | tf_op jit(solution)/shard_map/ppermute | solution.py:37
  21.2 29.9 %collective-permute-start.6 = (bf16[1,2,256,512]{3,2,1,0:T(8,128)(2,1)}, bf16[1,2,256,512]{3,2,1,0:T(8,128)(2,1)}, u32[]{:S(2)}, u32[]{:S(2)}) collective-permute-start(bf16[1,2,256,512]{3,2,1,0:T(8,128)(2,1)} %refs_0_.1), channel_id=1, source_target_pairs={{0,16},{8,24},{16,0},{24,8},{32,48},{40,56},{48,32},{56,40},{64,80... | collective-permute-start | bytes 1572872 | tf_op jit(solution)/shard_map/ppermute | solution.py:37
  32.8 24.7 %copy-start.1 = (bf16[1,2,256,512]{3,2,1,0:T(8,128)(2,1)}, bf16[1,2,256,512]{3,2,1,0:T(8,128)(2,1)S(1)}, u32[]{:S(2)}) copy-start(bf16[1,2,256,512]{3,2,1,0:T(8,128)(2,1)S(1)} %collective-permute-done.refs_1_) | copy-start | bytes 1572868
  32.9 18.3 %collective-permute-start.1 = (bf16[1,1,256,512]{3,2,1,0:T(8,128)(2,1)S(1)}, bf16[1,1,256,512]{3,2,1,0:T(8,128)(2,1)S(1)}, u32[]{:S(2)}, u32[]{:S(2)}) collective-permute-start(bf16[1,1,256,512]{3,2,1,0:T(8,128)(2,1)S(1)} %slice.20), channel_id=1, source_target_pairs={{0,32},{8,40},{16,48},{24,56},{32,64},{40,72},{48,80},{56,88},{64,... | collective-permute-start | bytes 786440 | tf_op jit(solution)/shard_map/ppermute | solution.py:37
  40.6 18.5 %copy-start.2 = (bf16[1,2,256,512]{3,2,1,0:T(8,128)(2,1)}, bf16[1,2,256,512]{3,2,1,0:T(8,128)(2,1)S(1)}, u32[]{:S(2)}) copy-start(bf16[1,2,256,512]{3,2,1,0:T(8,128)(2,1)S(1)} %collective-permute-done.2.refs_2_) | copy-start | bytes 1572868
  40.6 16.9 %collective-permute-start.3 = (bf16[1,1,256,512]{3,2,1,0:T(8,128)(2,1)S(1)}, bf16[1,1,256,512]{3,2,1,0:T(8,128)(2,1)S(1)}, u32[]{:S(2)}, u32[]{:S(2)}) collective-permute-start(bf16[1,1,256,512]{3,2,1,0:T(8,128)(2,1)S(1)} %slice.21), channel_id=1, source_target_pairs={{0,96},{8,104},{16,112},{24,120},{32,0},{40,8},{48,16},{56,24},{64... | collective-permute-start | bytes 786440 | tf_op jit(solution)/shard_map/ppermute | solution.py:37
  44.6 6.6 %copy-start.3 = (bf16[1,2,256,512]{3,2,1,0:T(8,128)(2,1)}, bf16[1,2,256,512]{3,2,1,0:T(8,128)(2,1)S(1)}, u32[]{:S(2)}) copy-start(bf16[1,2,256,512]{3,2,1,0:T(8,128)(2,1)S(1)} %collective-permute-done.4.refs_3_) | copy-start | bytes 1572868
  44.6 28.1 %collective-permute-start.7 = (bf16[2,2,256,512]{3,2,1,0:T(8,128)(2,1)S(1)}, bf16[2,2,256,512]{3,2,1,0:T(8,128)(2,1)}, u32[]{:S(2)}, u32[]{:S(2)}) collective-permute-start(bf16[2,2,256,512]{3,2,1,0:T(8,128)(2,1)S(1)} %constant_dynamic-update-slice_fusion), channel_id=1, source_target_pairs={{0,8},{8,16},{16,24},{24,0},{32,40},{40,48},{48,56},{56,32},{64,72... | collective-permute-start | bytes 3145736 | tf_op jit(solution)/shard_map/ppermute | solution.py:37
  48.0 3.1 %copy-start.4 = (bf16[1,2,256,512]{3,2,1,0:T(8,128)(2,1)}, bf16[1,2,256,512]{3,2,1,0:T(8,128)(2,1)S(1)}, u32[]{:S(2)}) copy-start(bf16[1,2,256,512]{3,2,1,0:T(8,128)(2,1)S(1)} %collective-permute-done.5.refs_4_) | copy-start | bytes 1572868
  48.0 28.1 %collective-permute-start.8 = (bf16[2,2,256,512]{3,2,1,0:T(8,128)(2,1)S(1)}, bf16[2,2,256,512]{3,2,1,0:T(8,128)(2,1)}, u32[]{:S(2)}, u32[]{:S(2)}) collective-permute-start(bf16[2,2,256,512]{3,2,1,0:T(8,128)(2,1)S(1)} %constant_dynamic-update-slice_fusion), channel_id=1, source_target_pairs={{0,24},{8,0},{16,8},{24,16},{32,56},{40,32},{48,40},{56,48},{64,88... | collective-permute-start | bytes 3145736 | tf_op jit(solution)/shard_map/ppermute | solution.py:37
  57.5 1.6 %copy-start = (bf16[1,2,256,512]{3,2,1,0:T(8,128)(2,1)}, bf16[1,2,256,512]{3,2,1,0:T(8,128)(2,1)S(1)}, u32[]{:S(2)}) copy-start(bf16[1,2,256,512]{3,2,1,0:T(8,128)(2,1)S(1)} %constant_dynamic-update-slice_fusion.2.refs_8_) | copy-start | bytes 1572868
  59.1 38.0 %all-to-all-start = ((bf16[4,2,256,512]{3,2,1,0:T(8,128)(2,1)}), bf16[4,2,256,512]{3,2,1,0:T(8,128)(2,1)}, u32[]{:S(2)}, u32[]{:S(2)}) async-start(bf16[4,2,256,512]{3,2,1,0:T(8,128)(2,1)} %broadcast_in_dim.14), calls=%async_computation | async-start | bytes 4194304 | tf_op jit(solution)/shard_map/all_to_all | solution.py:42
  64.2 21.4 %collective-permute-start.10 = (bf16[1,2,256,512]{3,2,1,0:T(8,128)(2,1)}, bf16[1,2,256,512]{3,2,1,0:T(8,128)(2,1)S(1)}, u32[]{:S(2)}, u32[]{:S(2)}) collective-permute-start(bf16[1,2,256,512]{3,2,1,0:T(8,128)(2,1)} %collective-permute-done.6.refs_5_), channel_id=1, source_target_pairs={{0,96},{8,104},{16,112},{24,120},{32,0},{40,8},{48,16},{56,24},{64... | collective-permute-start | bytes 1572872 | tf_op jit(solution)/shard_map/ppermute | solution.py:37
  68.4 27.8 %collective-permute-start.9 = (bf16[1,2,256,512]{3,2,1,0:T(8,128)(2,1)}, bf16[1,2,256,512]{3,2,1,0:T(8,128)(2,1)}, u32[]{:S(2)}, u32[]{:S(2)}) collective-permute-start(bf16[1,2,256,512]{3,2,1,0:T(8,128)(2,1)} %collective-permute-done.6.refs_5_), channel_id=1, source_target_pairs={{0,32},{8,40},{16,48},{24,56},{32,64},{40,72},{48,80},{56,88},{64,... | collective-permute-start | bytes 1572872 | tf_op jit(solution)/shard_map/ppermute | solution.py:37
  85.6 11.6 %copy-start.5 = (bf16[1,2,256,512]{3,2,1,0:T(8,128)(2,1)}, bf16[1,2,256,512]{3,2,1,0:T(8,128)(2,1)S(1)}, u32[]{:S(2)}) copy-start(bf16[1,2,256,512]{3,2,1,0:T(8,128)(2,1)S(1)} %collective-permute-done.10.refs_1_) | copy-start | bytes 1572868
Sparse Core Ops, SparseCore 0:
  9.4 55.8 all-gather.1

commit v5 on v4

--- a/solution.py
+++ b/solution.py
@@ -223,6 +223,28 @@
     )(weights, source, base, late_left, *arrays)
 
 
+def place_both(first, second, out, done):
+    copies = [
+        pltpu.make_async_copy(block.at[0], out.at[n], done.at[n])
+        for n, block in enumerate((first, second))
+    ]
+    for copy in copies:
+        copy.start()
+    for copy in copies:
+        copy.wait()
+
+
+def join(first, second):
+    return pl.pallas_call(
+        place_both,
+        out_shape=jax.ShapeDtypeStruct((2, 2, ROWS, COLS), jnp.bfloat16),
+        in_specs=[pl.BlockSpec(memory_space=pl.ANY)] * 2,
+        out_specs=pl.BlockSpec(memory_space=pl.ANY),
+        scratch_shapes=[pltpu.SemaphoreType.DMA((2,))],
+        cost_estimate=pl.CostEstimate(flops=0, bytes_accessed=1 << 21, transcendentals=0),
+    )(first, second)
+
+
 def shards(recorded, aperture):
     weights = tile_weights(aperture).reshape(8, NB)
     source = lax.axis_index("src")
@@ -236,7 +258,7 @@
     *across, before, after, opposite, weights = lax.optimization_barrier(
         (*across, before, after, opposite, weights)
     )
-    pair = jnp.concatenate([above, below], axis=0)
+    pair = join(above, below)
     pair_left, pair_right = shift(pair, 0, 1), shift(pair, 0, -1)
     far = jnp.concatenate(across, axis=1)
     across_line = along(far, X_LINES)

time: 110 us -> 144 us (1.31)
  the two profiles are of different devices: /device:TPU:386 before, /device:TPU:322 now
where the time goes in v5:
time: 144 us; the launch traced here: 143 us
  starting transfers between devices  47.9 us (33%)
  Pallas kernels  46.2 us (32%)
  waiting for transfers between devices  32.2 us (22%)
  between operations  13.6 us (9%)
  local copies, waits for them, and re-layouts  1.98 us (1%)
    ppermute x11, starting transfers between devices, shift(): return lax.ppermute(block, 'src', pairs)  41.7 us
    pallas_call x1, Pallas kernels, join(): pl.pallas_call(place_both, out_shape=jax.ShapeDtypeStruct((2, 2, ROWS, CO...  32.9 us
    ppermute x11, waiting for transfers between devices, shift(): return lax.ppermute(block, 'src', pairs)  23.2 us
    all_to_all x1, waiting for transfers between devices, along(): lax.all_to_all(copies, 'src', 0, 0, tiled=True, axis_index_groups=lines)  8.35 us
    pallas_call x1, Pallas kernels, add_early(): pl.pallas_call(functools.partial(sum_early, steps, late, 6), out_shape=(S...  8.15 us
    all_to_all x1, starting transfers between devices, along(): lax.all_to_all(copies, 'src', 0, 0, tiled=True, axis_index_groups=lines)  6.16 us
    pallas_call x1, Pallas kernels, add_late(): pl.pallas_call(functools.partial(sum_late, steps, 2), out_shape=SUM, in_s...  5.2 us
  transfers between devices with their start and end apart: 13, of which 7 were waited for; matrix products, arithmetic and copies ran while one was open for 2% of the time, Pallas kernels for 29%

profile of v5, /device:TPU:322, one launch (start us, length us, event | category | flops | bytes accessed | tf_op | source)
XLA Modules:
  0.0 143.3 jit_solution(16565314159083676992)
XLA Ops:
  6.5 0.7 all-gather.2.cloned.1.call-update
  7.3 4.5 %collective-permute-start = (bf16[1,2,256,512]{3,2,1,0:T(8,128)(2,1)}, bf16[1,2,256,512]{3,2,1,0:T(8,128)(2,1)S(1)}, u32[]{:S(2)}, u32[]{:S(2)}) collective-permute-start(bf16[1,2,256,512]{3,2,1,0:T(8,128)(2,1)} %refs_0_.1), channel_id=1, source_target_pairs={{0,32},{8,40},{16,48},{24,56},{32,64},{40,72},{48,80},{56,88},{64,... | collective-permute-start | bytes 1572872 | tf_op jit(solution)/shard_map/ppermute | solution.py:37
  11.8 3.6 %collective-permute-start.2 = (bf16[1,2,256,512]{3,2,1,0:T(8,128)(2,1)}, bf16[1,2,256,512]{3,2,1,0:T(8,128)(2,1)S(1)}, u32[]{:S(2)}, u32[]{:S(2)}) collective-permute-start(bf16[1,2,256,512]{3,2,1,0:T(8,128)(2,1)} %refs_0_.1), channel_id=1, source_target_pairs={{0,96},{8,104},{16,112},{24,120},{32,0},{40,8},{48,16},{56,24},{64... | collective-permute-start | bytes 1572872 | tf_op jit(solution)/shard_map/ppermute | solution.py:37
  15.4 3.4 %collective-permute-start.4 = (bf16[1,2,256,512]{3,2,1,0:T(8,128)(2,1)}, bf16[1,2,256,512]{3,2,1,0:T(8,128)(2,1)S(1)}, u32[]{:S(2)}, u32[]{:S(2)}) collective-permute-start(bf16[1,2,256,512]{3,2,1,0:T(8,128)(2,1)} %refs_0_.1), channel_id=1, source_target_pairs={{0,8},{8,16},{16,24},{24,0},{32,40},{40,48},{48,56},{56,32},{64,72... | collective-permute-start | bytes 1572872 | tf_op jit(solution)/shard_map/ppermute | solution.py:37
  18.8 2.4 %collective-permute-start.5 = (bf16[1,2,256,512]{3,2,1,0:T(8,128)(2,1)}, bf16[1,2,256,512]{3,2,1,0:T(8,128)(2,1)S(1)}, u32[]{:S(2)}, u32[]{:S(2)}) collective-permute-start(bf16[1,2,256,512]{3,2,1,0:T(8,128)(2,1)} %refs_0_.1), channel_id=1, source_target_pairs={{0,24},{8,0},{16,8},{24,16},{32,56},{40,32},{48,40},{56,48},{64,88... | collective-permute-start | bytes 1572872 | tf_op jit(solution)/shard_map/ppermute | solution.py:37
  21.2 4.0 %collective-permute-start.6 = (bf16[1,2,256,512]{3,2,1,0:T(8,128)(2,1)}, bf16[1,2,256,512]{3,2,1,0:T(8,128)(2,1)}, u32[]{:S(2)}, u32[]{:S(2)}) collective-permute-start(bf16[1,2,256,512]{3,2,1,0:T(8,128)(2,1)} %refs_0_.1), channel_id=1, source_target_pairs={{0,16},{8,24},{16,0},{24,8},{32,48},{40,56},{48,32},{56,40},{64,80... | collective-permute-start | bytes 1572872 | tf_op jit(solution)/shard_map/ppermute | solution.py:37
  25.3 7.6 %collective-permute-done.first.refs_1_ = bf16[1,2,256,512]{3,2,1,0:T(8,128)(2,1)S(1)} collective-permute-done((bf16[1,2,256,512]{3,2,1,0:T(8,128)(2,1)}, bf16[1,2,256,512]{3,2,1,0:T(8,128)(2,1)S(1)}, u32[]{:S(2)}, u32[]{:S(2)}) %collective-permute-start) | collective-permute-done | bytes 524320 | tf_op jit(solution)/shard_map/ppermute | solution.py:37
  32.9 7.2 %collective-permute-start.1 = (bf16[1,1,256,512]{3,2,1,0:T(8,128)(2,1)S(1)}, bf16[1,1,256,512]{3,2,1,0:T(8,128)(2,1)S(1)}, u32[]{:S(2)}, u32[]{:S(2)}) collective-permute-start(bf16[1,1,256,512]{3,2,1,0:T(8,128)(2,1)S(1)} %slice.20), channel_id=1, source_target_pairs={{0,32},{8,40},{16,48},{24,56},{32,64},{40,72},{48,80},{56,88},{64,... | collective-permute-start | bytes 786440 | tf_op jit(solution)/shard_map/ppermute | solution.py:37
  40.1 0.4 collective-permute-done.2.second.refs_2_
  40.6 3.9 %collective-permute-start.3 = (bf16[1,1,256,512]{3,2,1,0:T(8,128)(2,1)S(1)}, bf16[1,1,256,512]{3,2,1,0:T(8,128)(2,1)S(1)}, u32[]{:S(2)}, u32[]{:S(2)}) collective-permute-start(bf16[1,1,256,512]{3,2,1,0:T(8,128)(2,1)S(1)} %slice.21), channel_id=1, source_target_pairs={{0,96},{8,104},{16,112},{24,120},{32,0},{40,8},{48,16},{56,24},{64... | collective-permute-start | bytes 786440 | tf_op jit(solution)/shard_map/ppermute | solution.py:37
  44.5 0.7 fusion.8
  45.2 0.1 div.11
  45.3 0.1 lt.11
  45.4 0.1 sub.31
  45.5 0.1 sub.35
  45.5 32.9 %shard_map.28 = bf16[2,2,256,512]{3,2,1,0:T(8,128)(2,1)} custom-call(bf16[1,2,256,512]{3,2,1,0:T(8,128)(2,1)} %copy-done.1, bf16[1,2,256,512]{3,2,1,0:T(8,128)(2,1)} %copy-done.2), custom_call_target="tpu_custom_call" | custom-call | bytes 2097152 | tf_op jit(solution)/shard_map/pallas_call | solution.py:238
  78.4 0.0 collective-permute-done.4.refs_3_
  78.5 3.4 %collective-permute-start.7 = (bf16[2,2,256,512]{3,2,1,0:T(8,128)(2,1)}, bf16[2,2,256,512]{3,2,1,0:T(8,128)(2,1)}, u32[]{:S(2)}, u32[]{:S(2)}) collective-permute-start(bf16[2,2,256,512]{3,2,1,0:T(8,128)(2,1)} %shard_map.28), channel_id=1, source_target_pairs={{0,8},{8,16},{16,24},{24,0},{32,40},{40,48},{48,56},{56,32},{64,72... | collective-permute-start | bytes 3145736 | tf_op jit(solution)/shard_map/ppermute | solution.py:37
  81.9 0.0 collective-permute-done.5.refs_4_
  81.9 2.4 %collective-permute-start.8 = (bf16[2,2,256,512]{3,2,1,0:T(8,128)(2,1)}, bf16[2,2,256,512]{3,2,1,0:T(8,128)(2,1)}, u32[]{:S(2)}, u32[]{:S(2)}) collective-permute-start(bf16[2,2,256,512]{3,2,1,0:T(8,128)(2,1)} %shard_map.28), channel_id=1, source_target_pairs={{0,24},{8,0},{16,8},{24,16},{32,56},{40,32},{48,40},{56,48},{64,88... | collective-permute-start | bytes 3145736 | tf_op jit(solution)/shard_map/ppermute | solution.py:37
  84.3 0.7 fusion.4.weights
  85.1 1.6 %broadcast_in_dim.14 = bf16[4,2,256,512]{3,2,1,0:T(8,128)(2,1)} broadcast(bf16[2,256,512]{2,1,0:T(8,128)(2,1)S(1)} %bitcast.10), dimensions={1,2,3} | broadcast | bytes 2621440 | tf_op jit(solution)/shard_map/broadcast_in_dim | solution.py:41
  86.7 6.2 %all-to-all-start = ((bf16[4,2,256,512]{3,2,1,0:T(8,128)(2,1)}), bf16[4,2,256,512]{3,2,1,0:T(8,128)(2,1)}, u32[]{:S(2)}, u32[]{:S(2)}) async-start(bf16[4,2,256,512]{3,2,1,0:T(8,128)(2,1)} %broadcast_in_dim.14), calls=%async_computation | async-start | bytes 4194304 | tf_op jit(solution)/shard_map/all_to_all | solution.py:42
  92.8 4.0 %collective-permute-start.10 = (bf16[1,2,256,512]{3,2,1,0:T(8,128)(2,1)}, bf16[1,2,256,512]{3,2,1,0:T(8,128)(2,1)S(1)}, u32[]{:S(2)}, u32[]{:S(2)}) collective-permute-start(bf16[1,2,256,512]{3,2,1,0:T(8,128)(2,1)} %collective-permute-done.6.refs_5_), channel_id=1, source_target_pairs={{0,96},{8,104},{16,112},{24,120},{32,0},{40,8},{48,16},{56,24},{64... | collective-permute-start | bytes 1572872 | tf_op jit(solution)/shard_map/ppermute | solution.py:37
  96.8 2.8 %collective-permute-start.9 = (bf16[1,2,256,512]{3,2,1,0:T(8,128)(2,1)}, bf16[1,2,256,512]{3,2,1,0:T(8,128)(2,1)}, u32[]{:S(2)}, u32[]{:S(2)}) collective-permute-start(bf16[1,2,256,512]{3,2,1,0:T(8,128)(2,1)} %collective-permute-done.6.refs_5_), channel_id=1, source_target_pairs={{0,32},{8,40},{16,48},{24,56},{32,64},{40,72},{48,80},{56,88},{64,... | collective-permute-start | bytes 1572872 | tf_op jit(solution)/shard_map/ppermute | solution.py:37
  99.6 7.2 %collective-permute-done.7.refs_6_ = bf16[2,2,256,512]{3,2,1,0:T(8,128)(2,1)} collective-permute-done((bf16[2,2,256,512]{3,2,1,0:T(8,128)(2,1)}, bf16[2,2,256,512]{3,2,1,0:T(8,128)(2,1)}, u32[]{:S(2)}, u32[]{:S(2)}) %collective-permute-start.7) | collective-permute-done | bytes 1048608 | tf_op jit(solution)/shard_map/ppermute | solution.py:37
  106.8 3.4 %collective-permute-done.8.refs_7_ = bf16[2,2,256,512]{3,2,1,0:T(8,128)(2,1)} collective-permute-done((bf16[2,2,256,512]{3,2,1,0:T(8,128)(2,1)}, bf16[2,2,256,512]{3,2,1,0:T(8,128)(2,1)}, u32[]{:S(2)}, u32[]{:S(2)}) %collective-permute-start.8) | collective-permute-done | bytes 1048608 | tf_op jit(solution)/shard_map/ppermute | solution.py:37
  110.2 8.2 %shard_map.29 = (f32[1,2,256,512]{3,2,1,0:T(8,128)}, bf16[5,2,256,256]{3,2,1,0:T(8,128)(2,1)}) custom-call(f32[8,32]{1,0:T(8,128)} %fusion.4.weights, s32[1]{0:T(128)} %bitcast.source, bf16[1,2,256,4096]{3,2,1,0:T(8,128)(2,1)} %all-gather.2.cloned.1.call-done.left, bf16[1,2,256,512]{3,2,1,0:T(8,128)(2,1)} %refs_0_.1, bf16[1,2,256,512]{3,2,1,0:T(8,128)(2,1)} %copy-done.1, ...), custom_call_target="tpu_custom_call" | custom-call | flops 8858370048 | bytes 10747904 | tf_op jit(solution)/shard_map/pallas_call | solution.py:187
  118.4 0.9 collective-permute-done.10.refs_1_
  119.3 3.6 %collective-permute-done.9.refs_0_ = bf16[1,2,256,512]{3,2,1,0:T(8,128)(2,1)} collective-permute-done((bf16[1,2,256,512]{3,2,1,0:T(8,128)(2,1)}, bf16[1,2,256,512]{3,2,1,0:T(8,128)(2,1)}, u32[]{:S(2)}, u32[]{:S(2)}) %collective-permute-start.9) | collective-permute-done | bytes 524320 | tf_op jit(solution)/shard_map/ppermute | solution.py:37
  122.9 8.4 %all-to-all-done.refs_2_ = bf16[4,2,256,512]{3,2,1,0:T(8,128)(2,1)} async-done(((bf16[4,2,256,512]{3,2,1,0:T(8,128)(2,1)}), bf16[4,2,256,512]{3,2,1,0:T(8,128)(2,1)}, u32[]{:S(2)}, u32[]{:S(2)}) %all-to-all-start) | async-done | bytes 2097184 | tf_op jit(solution)/shard_map/all_to_all | solution.py:42
  131.2 5.2 %shard_map.30 = f32[1,2,256,512]{3,2,1,0:T(8,128)} custom-call(f32[8,32]{1,0:T(8,128)} %fusion.4.weights, s32[1]{0:T(128)} %bitcast.source, f32[1,2,256,512]{3,2,1,0:T(8,128)} %get-tuple-element.19.base, bf16[5,2,256,256]{3,2,1,0:T(8,128)(2,1)} %get-tuple-element.20.late_left, bf16[1,2,256,512]{3,2,1,0:T(8,128)(2,1)} %collective-permute-done.9.refs_0_, ...), custom_call_target="tpu_custom_call" | custom-call | flops 4026531840 | bytes 6029312 | tf_op jit(solution)/shard_map/pallas_call | solution.py:206
  (21 shorter events, 0.1 us)
Async XLA Ops:
  6.5 103.7 %all-gather.2.cloned.1.call-start = ((), (), s32[]{:S(2)}) async-start(), calls=%async_computation.1 | async-start | bytes 4718592 | tf_op jit(solution)/shard_map/all_gather | solution.py:253
  7.3 25.6 %collective-permute-start = (bf16[1,2,256,512]{3,2,1,0:T(8,128)(2,1)}, bf16[1,2,256,512]{3,2,1,0:T(8,128)(2,1)S(1)}, u32[]{:S(2)}, u32[]{:S(2)}) collective-permute-start(bf16[1,2,256,512]{3,2,1,0:T(8,128)(2,1)} %refs_0_.1), channel_id=1, source_target_pairs={{0,32},{8,40},{16,48},{24,56},{32,64},{40,72},{48,80},{56,88},{64,... | collective-permute-start | bytes 1572872 | tf_op jit(solution)/shard_map/ppermute | solution.py:37
  11.8 28.8 %collective-permute-start.2 = (bf16[1,2,256,512]{3,2,1,0:T(8,128)(2,1)}, bf16[1,2,256,512]{3,2,1,0:T(8,128)(2,1)S(1)}, u32[]{:S(2)}, u32[]{:S(2)}) collective-permute-start(bf16[1,2,256,512]{3,2,1,0:T(8,128)(2,1)} %refs_0_.1), channel_id=1, source_target_pairs={{0,96},{8,104},{16,112},{24,120},{32,0},{40,8},{48,16},{56,24},{64... | collective-permute-start | bytes 1572872 | tf_op jit(solution)/shard_map/ppermute | solution.py:37
  15.4 63.1 %collective-permute-start.4 = (bf16[1,2,256,512]{3,2,1,0:T(8,128)(2,1)}, bf16[1,2,256,512]{3,2,1,0:T(8,128)(2,1)S(1)}, u32[]{:S(2)}, u32[]{:S(2)}) collective-permute-start(bf16[1,2,256,512]{3,2,1,0:T(8,128)(2,1)} %refs_0_.1), channel_id=1, source_target_pairs={{0,8},{8,16},{16,24},{24,0},{32,40},{40,48},{48,56},{56,32},{64,72... | collective-permute-start | bytes 1572872 | tf_op jit(solution)/shard_map/ppermute | solution.py:37
  18.8 63.1 %collective-permute-start.5 = (bf16[1,2,256,512]{3,2,1,0:T(8,128)(2,1)}, bf16[1,2,256,512]{3,2,1,0:T(8,128)(2,1)S(1)}, u32[]{:S(2)}, u32[]{:S(2)}) collective-permute-start(bf16[1,2,256,512]{3,2,1,0:T(8,128)(2,1)} %refs_0_.1), channel_id=1, source_target_pairs={{0,24},{8,0},{16,8},{24,16},{32,56},{40,32},{48,40},{56,48},{64,88... | collective-permute-start | bytes 1572872 | tf_op jit(solution)/shard_map/ppermute | solution.py:37
  21.2 63.8 %collective-permute-start.6 = (bf16[1,2,256,512]{3,2,1,0:T(8,128)(2,1)}, bf16[1,2,256,512]{3,2,1,0:T(8,128)(2,1)}, u32[]{:S(2)}, u32[]{:S(2)}) collective-permute-start(bf16[1,2,256,512]{3,2,1,0:T(8,128)(2,1)} %refs_0_.1), channel_id=1, source_target_pairs={{0,16},{8,24},{16,0},{24,8},{32,48},{40,56},{48,32},{56,40},{64,80... | collective-permute-start | bytes 1572872 | tf_op jit(solution)/shard_map/ppermute | solution.py:37
  32.8 12.7 %copy-start.1 = (bf16[1,2,256,512]{3,2,1,0:T(8,128)(2,1)}, bf16[1,2,256,512]{3,2,1,0:T(8,128)(2,1)S(1)}, u32[]{:S(2)}) copy-start(bf16[1,2,256,512]{3,2,1,0:T(8,128)(2,1)S(1)} %collective-permute-done.first.refs_1_) | copy-start | bytes 1572868
  32.9 52.2 %collective-permute-start.1 = (bf16[1,1,256,512]{3,2,1,0:T(8,128)(2,1)S(1)}, bf16[1,1,256,512]{3,2,1,0:T(8,128)(2,1)S(1)}, u32[]{:S(2)}, u32[]{:S(2)}) collective-permute-start(bf16[1,1,256,512]{3,2,1,0:T(8,128)(2,1)S(1)} %slice.20), channel_id=1, source_target_pairs={{0,32},{8,40},{16,48},{24,56},{32,64},{40,72},{48,80},{56,88},{64,... | collective-permute-start | bytes 786440 | tf_op jit(solution)/shard_map/ppermute | solution.py:37
  40.6 5.0 %copy-start.2 = (bf16[1,2,256,512]{3,2,1,0:T(8,128)(2,1)}, bf16[1,2,256,512]{3,2,1,0:T(8,128)(2,1)S(1)}, u32[]{:S(2)}) copy-start(bf16[1,2,256,512]{3,2,1,0:T(8,128)(2,1)S(1)} %collective-permute-done.2.second.refs_2_) | copy-start | bytes 1572868
  40.6 44.5 %collective-permute-start.3 = (bf16[1,1,256,512]{3,2,1,0:T(8,128)(2,1)S(1)}, bf16[1,1,256,512]{3,2,1,0:T(8,128)(2,1)S(1)}, u32[]{:S(2)}, u32[]{:S(2)}) collective-permute-start(bf16[1,1,256,512]{3,2,1,0:T(8,128)(2,1)S(1)} %slice.21), channel_id=1, source_target_pairs={{0,96},{8,104},{16,112},{24,120},{32,0},{40,8},{48,16},{56,24},{64... | collective-permute-start | bytes 786440 | tf_op jit(solution)/shard_map/ppermute | solution.py:37
  78.5 6.6 %copy-start.3 = (bf16[1,2,256,512]{3,2,1,0:T(8,128)(2,1)}, bf16[1,2,256,512]{3,2,1,0:T(8,128)(2,1)S(1)}, u32[]{:S(2)}) copy-start(bf16[1,2,256,512]{3,2,1,0:T(8,128)(2,1)S(1)} %collective-permute-done.4.refs_3_) | copy-start | bytes 1572868
  78.5 28.3 %collective-permute-start.7 = (bf16[2,2,256,512]{3,2,1,0:T(8,128)(2,1)}, bf16[2,2,256,512]{3,2,1,0:T(8,128)(2,1)}, u32[]{:S(2)}, u32[]{:S(2)}) collective-permute-start(bf16[2,2,256,512]{3,2,1,0:T(8,128)(2,1)} %shard_map.28), channel_id=1, source_target_pairs={{0,8},{8,16},{16,24},{24,0},{32,40},{40,48},{48,56},{56,32},{64,72... | collective-permute-start | bytes 3145736 | tf_op jit(solution)/shard_map/ppermute | solution.py:37
  81.9 3.1 %copy-start.4 = (bf16[1,2,256,512]{3,2,1,0:T(8,128)(2,1)}, bf16[1,2,256,512]{3,2,1,0:T(8,128)(2,1)S(1)}, u32[]{:S(2)}) copy-start(bf16[1,2,256,512]{3,2,1,0:T(8,128)(2,1)S(1)} %collective-permute-done.5.refs_4_) | copy-start | bytes 1572868
  81.9 28.3 %collective-permute-start.8 = (bf16[2,2,256,512]{3,2,1,0:T(8,128)(2,1)}, bf16[2,2,256,512]{3,2,1,0:T(8,128)(2,1)}, u32[]{:S(2)}, u32[]{:S(2)}) collective-permute-start(bf16[2,2,256,512]{3,2,1,0:T(8,128)(2,1)} %shard_map.28), channel_id=1, source_target_pairs={{0,24},{8,0},{16,8},{24,16},{32,56},{40,32},{48,40},{56,48},{64,88... | collective-permute-start | bytes 3145736 | tf_op jit(solution)/shard_map/ppermute | solution.py:37
  85.1 1.6 %copy-start = (bf16[1,2,256,512]{3,2,1,0:T(8,128)(2,1)}, bf16[1,2,256,512]{3,2,1,0:T(8,128)(2,1)S(1)}, u32[]{:S(2)}) copy-start(bf16[1,2,256,512]{3,2,1,0:T(8,128)(2,1)S(1)} %constant_dynamic-update-slice_fusion.refs_8_) | copy-start | bytes 1572868
  86.7 44.5 %all-to-all-start = ((bf16[4,2,256,512]{3,2,1,0:T(8,128)(2,1)}), bf16[4,2,256,512]{3,2,1,0:T(8,128)(2,1)}, u32[]{:S(2)}, u32[]{:S(2)}) async-start(bf16[4,2,256,512]{3,2,1,0:T(8,128)(2,1)} %broadcast_in_dim.14), calls=%async_computation | async-start | bytes 4194304 | tf_op jit(solution)/shard_map/all_to_all | solution.py:42
  92.8 26.4 %collective-permute-start.10 = (bf16[1,2,256,512]{3,2,1,0:T(8,128)(2,1)}, bf16[1,2,256,512]{3,2,1,0:T(8,128)(2,1)S(1)}, u32[]{:S(2)}, u32[]{:S(2)}) collective-permute-start(bf16[1,2,256,512]{3,2,1,0:T(8,128)(2,1)} %collective-permute-done.6.refs_5_), channel_id=1, source_target_pairs={{0,96},{8,104},{16,112},{24,120},{32,0},{40,8},{48,16},{56,24},{64... | collective-permute-start | bytes 1572872 | tf_op jit(solution)/shard_map/ppermute | solution.py:37
  96.8 26.1 %collective-permute-start.9 = (bf16[1,2,256,512]{3,2,1,0:T(8,128)(2,1)}, bf16[1,2,256,512]{3,2,1,0:T(8,128)(2,1)}, u32[]{:S(2)}, u32[]{:S(2)}) collective-permute-start(bf16[1,2,256,512]{3,2,1,0:T(8,128)(2,1)} %collective-permute-done.6.refs_5_), channel_id=1, source_target_pairs={{0,32},{8,40},{16,48},{24,56},{32,64},{40,72},{48,80},{56,88},{64,... | collective-permute-start | bytes 1572872 | tf_op jit(solution)/shard_map/ppermute | solution.py:37
  119.3 11.9 %copy-start.5 = (bf16[1,2,256,512]{3,2,1,0:T(8,128)(2,1)}, bf16[1,2,256,512]{3,2,1,0:T(8,128)(2,1)S(1)}, u32[]{:S(2)}) copy-start(bf16[1,2,256,512]{3,2,1,0:T(8,128)(2,1)S(1)} %collective-permute-done.10.refs_1_) | copy-start | bytes 1572868
Sparse Core Ops, SparseCore 0:
  9.4 56.5 all-gather.1
